TPU v7x, 1024 devices: a whole 4x4x32 slice. The times are simulated.
1024 devices in a mesh: dom: 64 (over z, core), grp: 16 (over y, x).
Axes of the slice: x: 4, y: 4, z: 32, core: 2. Of those that a mesh axis runs over, the one named last changes fastest.
Arguments:
- forcing: float32 [12288, 135], P(('dom', 'grp')), may hold values from -6 to 6
- diag_blocks: bfloat16 [12288, 135, 135], P(('dom', 'grp')), as said below
- off_blocks: bfloat16 [12288, 6, 135, 135], P(('dom', 'grp')), may hold values from -0.125 to 0.125
- precond: bfloat16 [12288, 135, 135], P(('dom', 'grp')), as said below
- face_part: int32 [6, 12288], P(None, ('dom', 'grp')), may hold values from -1 to 63, as said below
- face_slot: int32 [6, 12288], P(None, ('dom', 'grp')), may hold values from 0 to 191, as said below
- row_perm: int32 [64, 192], P('dom'), may hold values from 0 to 191, as said below
Outputs:
- adjoint: float32 [12288, 135], P(('dom', 'grp'))
- residual: float32 [12288, 135], P(('dom', 'grp'))
Inputs may be any that keep to these rules, and one draw needn't show every extreme that they name: `face_part`: each entry is -1 (a wall) or the partition of the face's neighbour, which is the element's own partition or the one just below or just above it in number; no face points below partition 0 or above 63. `face_slot`: block row of the neighbour in its own partition; read only where face_part is not -1. `row_perm`: each row is a permutation of 0 to 191. `diag_blocks`: dominant diagonal of 1 to 2 on every block. `precond`: dominant diagonal of 0.4 to 0.8 on every block.
All inputs are finite; a program needn't handle non-finite values.
Results may differ from a plain program's by a relative error of at most 0.012.
The roundings to bfloat16 on the way count: a program that leaves them out, or rounds other values in their place, can miss the bound.
Values sent between devices are 32-bit elements; how exact they have to be, the bound alone decides.
No kernel may reach another device: no remote copies, remote signals or barrier semaphores. Data moves between devices by JAX's collectives and lax.ppermute only.
A program may use at most 32 MiB of HBM per device.

v0:
```python
import jax
import jax.numpy as jnp
from jax import lax
from jax.sharding import PartitionSpec as P

ITERS = 2


def passed_along(block, axis, distance):
    devices = range(lax.axis_size(axis))
    route = [(i - distance, i) for i in devices if i - distance in devices]
    return lax.ppermute(block, axis, route)


def apply_precond(precond, vector):
    return jnp.einsum(
        "eij,ei->ej", precond, vector.astype(jnp.bfloat16), preferred_element_type=jnp.float32
    )


def shards(forcing, diag_blocks, off_blocks, precond, face_part, face_slot, row_perm):
    local_rows = forcing.shape[0]
    node_width = forcing.shape[1]
    group_size = lax.axis_size("grp")
    part_rows = local_rows * group_size
    my_part = lax.axis_index("dom")
    my_rank = lax.axis_index("grp")
    perm_row = row_perm[0]
    offset = face_part - my_part
    wall = face_part < 0
    dest = (offset + 1) * part_rows + face_slot
    dest = jnp.where(wall, -1, dest).reshape(-1)
    scatter_table = (dest[:, None] == jnp.arange(3 * part_rows, dtype=jnp.int32)[None, :]).astype(
        jnp.float32
    )
    owned = my_rank * local_rows + jnp.arange(local_rows, dtype=jnp.int32)
    adjoint = apply_precond(precond, forcing)
    residual = forcing
    for step in range(ITERS):
        adjoint_b = adjoint.astype(jnp.bfloat16)
        diag_term = jnp.einsum(
            "eij,ei->ej", diag_blocks, adjoint_b, preferred_element_type=jnp.float32
        )
        face_term = jnp.einsum(
            "ekij,ei->kej", off_blocks, adjoint_b, preferred_element_type=jnp.float32
        )
        face_term = face_term.reshape(-1, node_width)
        buffers = jnp.einsum("fp,fn->pn", scatter_table, face_term, precision=lax.Precision.HIGHEST)
        buffers = buffers.reshape(3, part_rows, node_width)
        from_prev = passed_along(buffers[2], "dom", 1)
        from_next = passed_along(buffers[0], "dom", -1)
        total = buffers[1] + from_prev + from_next
        share = lax.psum_scatter(total, "grp", scatter_dimension=0, tiled=True)
        select = (perm_row[None, :] == owned[:, None]).astype(jnp.float32)
        gathered = jnp.dot(
            select,
            lax.all_gather(share, "grp", axis=0, tiled=True),
            precision=lax.Precision.HIGHEST,
        )
        residual = forcing - (diag_term + gathered)
        adjoint = adjoint + apply_precond(precond, residual)
    return (adjoint, residual)


def solution(mesh):
    return jax.shard_map(
        shards,
        mesh=mesh,
        in_specs=(
            P(("dom", "grp"), None),
            P(("dom", "grp"), None, None),
            P(("dom", "grp"), None, None, None),
            P(("dom", "grp"), None, None),
            P(None, ("dom", "grp")),
            P(None, ("dom", "grp")),
            P("dom", None),
        ),
        out_specs=(P(("dom", "grp"), None), P(("dom", "grp"), None)),
        check_vma=False,
    )
```

profile of v0, /device:TPU:1, one launch (start us, length us, event | category | flops | bytes accessed | tf_op | source)
XLA Modules:
  0.0 405.1 jit_solution(17105537647816011489)
XLA Ops:
  7.2 0.0 copy-start
  7.2 0.0 copy-start.2
  7.2 0.0 copy-start.6
  7.2 0.0 copy-start.5
  7.2 0.0 copy-start.1
  7.2 0.0 copy-start.4
  7.2 0.0 all-reduce.5.cloned.1.call-start
  7.3 0.8 convert_bitcast_fusion.1
  8.1 0.5 copy-done
  8.6 0.2 fusion.24
  8.8 3.3 fusion.20
  12.2 0.0 copy-done.6
  12.2 0.0 copy-done.5
  12.2 0.1 eq.20
  12.3 0.4 fusion.5
  12.7 4.9 %collective-permute-start = (f32[192,135]{0,1:T(8,128)S(1)}, f32[192,135]{0,1:T(8,128)S(1)}, u32[]{:S(2)}, u32[]{:S(2)}) collective-permute-start(f32[192,135]{0,1:T(8,128)S(1)} %get-tuple-element.4), channel_id=1, source_target_pairs={{0,16},{16,32},{32,48},{48,64},{64,80},{80,96},{96,112},{112,128},... | collective-permute-start | bytes 311048 | tf_op jit(solution)/shard_map/ppermute | solution.py:12
  17.6 12.4 %collective-permute-start.1 = (f32[192,135]{0,1:T(8,128)S(1)}, f32[192,135]{0,1:T(8,128)S(1)}, u32[]{:S(2)}, u32[]{:S(2)}) collective-permute-start(f32[192,135]{0,1:T(8,128)S(1)} %get-tuple-element.5), channel_id=1, source_target_pairs={{16,0},{32,16},{48,32},{64,48},{80,64},{96,80},{112,96},{128,112},... | collective-permute-start | bytes 311048 | tf_op jit(solution)/shard_map/ppermute | solution.py:12
  30.0 0.0 copy-done.1
  30.1 0.2 fusion.22
  30.3 1.3 dynamic-slice
  32.2 0.0 collective-permute-done
  32.2 0.0 collective-permute-done.1
  32.2 0.8 fusion.7
  33.0 0.0 all-reduce.5.cloned.1.call-update
  33.0 0.0 all-reduce.7.cloned.1.call-start
  33.1 153.0 %all-reduce.5.cloned.1.call-done = f32[192,135]{0,1:T(8,128)} async-done(((f32[192,135]{0,1:T(8,128)}), f32[192,135]{0,1:T(8,128)}) %all-reduce.5.cloned.1.call-update) | async-done | bytes 103696
  186.1 1.0 dynamic-slice_bitcast_fusion.1
  187.1 0.1 copy.11
  187.1 16.7 %all-gather = f32[16,12,135]{2,1,0:T(8,128)S(1)} all-gather(f32[1,12,135]{2,1,0:T(8,128)S(1)} %copy.11), channel_id=1, replica_groups=mesh['dom'=64,'grp'=16] {'grp'}, dimensions={0}, use_global_device_ids=true | all-gather | bytes 110160 | tf_op jit(solution)/shard_map/all_gather | solution.py:57
  203.9 0.2 fusion.3
  204.1 0.3 fusion.18
  204.4 3.3 fusion.14
  207.7 0.4 fusion.4
  208.1 10.8 %collective-permute-start.2 = (f32[192,135]{0,1:T(8,128)S(1)}, f32[192,135]{0,1:T(8,128)S(1)}, u32[]{:S(2)}, u32[]{:S(2)}) collective-permute-start(f32[192,135]{0,1:T(8,128)S(1)} %get-tuple-element.2), channel_id=1, source_target_pairs={{0,16},{16,32},{32,48},{48,64},{64,80},{80,96},{96,112},{112,128},... | collective-permute-start | bytes 311048 | tf_op jit(solution)/shard_map/ppermute | solution.py:12
  218.9 1.9 collective-permute-start.3
  220.9 0.1 collective-permute-done.2
  220.9 4.4 %collective-permute-done.3 = f32[192,135]{0,1:T(8,128)S(1)} collective-permute-done((f32[192,135]{0,1:T(8,128)S(1)}, f32[192,135]{0,1:T(8,128)S(1)}, u32[]{:S(2)}, u32[]{:S(2)}) %collective-permute-start.3) | collective-permute-done | bytes 103712 | tf_op jit(solution)/shard_map/ppermute | solution.py:12
  225.3 0.8 fusion.6
  226.1 0.0 all-reduce.7.cloned.1.call-update
  226.1 0.2 fusion.16
  226.3 153.0 %all-reduce.7.cloned.1.call-done = f32[192,135]{0,1:T(8,128)} async-done(((f32[192,135]{0,1:T(8,128)}), f32[192,135]{0,1:T(8,128)}) %all-reduce.7.cloned.1.call-update) | async-done | bytes 103696
  379.4 1.0 dynamic-slice_bitcast_fusion
  380.3 0.1 copy.12
  380.4 16.7 %all-gather.1 = f32[16,12,135]{2,1,0:T(8,128)S(1)} all-gather(f32[1,12,135]{2,1,0:T(8,128)S(1)} %copy.12), channel_id=1, replica_groups=mesh['dom'=64,'grp'=16] {'grp'}, dimensions={0}, use_global_device_ids=true | all-gather | bytes 110160 | tf_op jit(solution)/shard_map/all_gather | solution.py:57
  397.2 0.2 fusion
  397.4 0.0 copy-start.3
  397.4 0.2 fusion.12
  397.7 0.6 bitcast_add_fusion
  (16 shorter events, 0.2 us)
Async XLA Ops:
  7.2 1.5 copy-start
  7.2 196.7 %copy-start.2 = (f32[12,135]{1,0:T(8,128)S(1)}, f32[12,135]{1,0:T(8,128)}, u32[]{:S(2)}) copy-start(f32[12,135]{1,0:T(8,128)} %param.7) | copy-start | bytes 19444
  7.2 5.0 %copy-start.6 = (s32[6,12]{1,0:T(8,128)S(1)}, s32[6,12]{1,0:T(8,128)}, u32[]{:S(2)}) copy-start(s32[6,12]{1,0:T(8,128)} %param.11) | copy-start | bytes 868
  7.2 5.0 %copy-start.5 = (s32[6,12]{1,0:T(8,128)S(1)}, s32[6,12]{1,0:T(8,128)}, u32[]{:S(2)}) copy-start(s32[6,12]{1,0:T(8,128)} %param.12) | copy-start | bytes 868
  7.2 22.8 %copy-start.1 = (bf16[12,135,135]{2,1,0:T(8,128)(2,1)S(1)}, bf16[12,135,135]{2,1,0:T(8,128)(2,1)}, u32[]{:S(2)}) copy-start(bf16[12,135,135]{2,1,0:T(8,128)(2,1)} %param.8) | copy-start | bytes 1312204
  7.2 196.7 %copy-start.4 = (s32[1,192]{1,0:T(1,128)S(1)}, s32[1,192]{1,0:T(1,128)}, u32[]{:S(2)}) copy-start(s32[1,192]{1,0:T(1,128)} %param.13) | copy-start | bytes 2308
  7.2 178.8 %all-reduce.5.cloned.1.call-start = ((), (), s32[]{:S(2)}) async-start(), calls=%async_computation | async-start | bytes 278528
  12.7 19.5 %collective-permute-start = (f32[192,135]{0,1:T(8,128)S(1)}, f32[192,135]{0,1:T(8,128)S(1)}, u32[]{:S(2)}, u32[]{:S(2)}) collective-permute-start(f32[192,135]{0,1:T(8,128)S(1)} %get-tuple-element.4), channel_id=1, source_target_pairs={{0,16},{16,32},{32,48},{48,64},{64,80},{80,96},{96,112},{112,128},... | collective-permute-start | bytes 311048 | tf_op jit(solution)/shard_map/ppermute | solution.py:12
  17.6 14.6 %collective-permute-start.1 = (f32[192,135]{0,1:T(8,128)S(1)}, f32[192,135]{0,1:T(8,128)S(1)}, u32[]{:S(2)}, u32[]{:S(2)}) collective-permute-start(f32[192,135]{0,1:T(8,128)S(1)} %get-tuple-element.5), channel_id=1, source_target_pairs={{16,0},{32,16},{48,32},{64,48},{80,64},{96,80},{112,96},{128,112},... | collective-permute-start | bytes 311048 | tf_op jit(solution)/shard_map/ppermute | solution.py:12
  33.0 346.3 %all-reduce.7.cloned.1.call-start = ((), (), s32[]{:S(2)}) async-start(), calls=%async_computation.1 | async-start | bytes 278528
  208.1 12.8 %collective-permute-start.2 = (f32[192,135]{0,1:T(8,128)S(1)}, f32[192,135]{0,1:T(8,128)S(1)}, u32[]{:S(2)}, u32[]{:S(2)}) collective-permute-start(f32[192,135]{0,1:T(8,128)S(1)} %get-tuple-element.2), channel_id=1, source_target_pairs={{0,16},{16,32},{32,48},{48,64},{64,80},{80,96},{96,112},{112,128},... | collective-permute-start | bytes 311048 | tf_op jit(solution)/shard_map/ppermute | solution.py:12
  218.9 6.4 %collective-permute-start.3 = (f32[192,135]{0,1:T(8,128)S(1)}, f32[192,135]{0,1:T(8,128)S(1)}, u32[]{:S(2)}, u32[]{:S(2)}) collective-permute-start(f32[192,135]{0,1:T(8,128)S(1)} %get-tuple-element.3), channel_id=1, source_target_pairs={{16,0},{32,16},{48,32},{64,48},{80,64},{96,80},{112,96},{128,112},... | collective-permute-start | bytes 311048 | tf_op jit(solution)/shard_map/ppermute | solution.py:12
  397.4 0.9 copy-start.3
Sparse Core Ops, SparseCore 0:
  33.1 152.8 all-reduce.4
  226.2 153.0 all-reduce.6
where the time goes:
time: 412 us; the launch traced here: 405 us
  waiting for transfers between devices  310 us (75%)
  blocking collectives  33.5 us (8%)
  starting transfers between devices  30.1 us (7%)
  between operations  15 us (4%)
  matrix products  8.88 us (2%)
  local copies, waits for them, and re-layouts  4.19 us (1%)
    unnamed x4, waiting for transfers between devices  306 us
    all_gather x2, blocking collectives, shards(): lax.all_gather(share, 'grp', axis=0, tiled=True)  33.5 us
    ppermute x4, starting transfers between devices, passed_along(): return lax.ppermute(block, axis, route)  30 us
  transfers between devices with their start and end apart: 6, of which 4 were waited for; matrix products, arithmetic and copies ran while one was open for 0% of the time, Pallas kernels for 0%

commit v1 on v0

v1 whole, which is shorter than its diff:
```python
import jax
import jax.numpy as jnp
from jax import lax
from jax.sharding import PartitionSpec as P

ITERS = 2
LANES = 256
SLOT_ROWS = 16


def passed_along(block, axis, distance):
    devices = range(lax.axis_size(axis))
    route = [(i - distance, i) for i in devices if i - distance in devices]
    return lax.ppermute(block, axis, route)


def apply_blocks(blocks, vector):
    return jnp.einsum(
        "eij,ei->ej", blocks, vector.astype(jnp.bfloat16), preferred_element_type=jnp.float32
    )


def shards(forcing, diag_blocks, off_blocks, precond, face_part, face_slot, row_perm):
    local_rows = forcing.shape[0]
    node_width = forcing.shape[1]
    group_size = lax.axis_size("grp")
    part_rows = local_rows * group_size
    my_part = lax.axis_index("dom")
    perm_row = row_perm[0]
    offset = face_part - my_part
    dest = (offset + 1) * part_rows + face_slot
    dest = jnp.where(face_part < 0, -1, dest).reshape(-1)
    scatter_table = (dest[:, None] == jnp.arange(3 * part_rows, dtype=jnp.int32)[None, :]).astype(
        jnp.float32
    )
    place = (perm_row // local_rows) * SLOT_ROWS + perm_row % local_rows
    place_table = (
        jnp.arange(group_size * SLOT_ROWS, dtype=jnp.int32)[:, None] == place[None, :]
    ).astype(jnp.float32)
    adjoint = apply_blocks(precond, forcing)
    residual = forcing
    for step in range(ITERS):
        adjoint_b = adjoint.astype(jnp.bfloat16)
        face_term = jnp.einsum(
            "ekij,ei->kej", off_blocks, adjoint_b, preferred_element_type=jnp.float32
        )
        face_term = face_term.reshape(-1, node_width)
        face_term = jnp.pad(face_term, ((0, 0), (0, LANES - node_width)))
        buffers = jnp.einsum("fp,fn->pn", scatter_table, face_term, precision=lax.Precision.HIGHEST)
        buffers = buffers.reshape(3, part_rows, LANES)
        from_prev = passed_along(buffers[2], "dom", 1)
        from_next = passed_along(buffers[0], "dom", -1)
        total = buffers[1] + from_prev + from_next
        outgoing = jnp.dot(place_table, total, precision=lax.Precision.HIGHEST)
        incoming = lax.all_to_all(
            outgoing.reshape(group_size, SLOT_ROWS, LANES), "grp", split_axis=0, concat_axis=0
        )
        gathered = jnp.sum(incoming, axis=0)[:local_rows, :node_width]
        diag_term = apply_blocks(diag_blocks, adjoint)
        residual = forcing - (diag_term + gathered)
        adjoint = adjoint + apply_blocks(precond, residual)
    return (adjoint, residual)


def solution(mesh):
    return jax.shard_map(
        shards,
        mesh=mesh,
        in_specs=(
            P(("dom", "grp"), None),
            P(("dom", "grp"), None, None),
            P(("dom", "grp"), None, None, None),
            P(("dom", "grp"), None, None),
            P(None, ("dom", "grp")),
            P(None, ("dom", "grp")),
            P("dom", None),
        ),
        out_specs=(P(("dom", "grp"), None), P(("dom", "grp"), None)),
        check_vma=False,
    )
```

time: 412 us -> 65.7 us (0.16)
  the two profiles are of different devices: /device:TPU:1 before, /device:TPU:97 now
where the time goes in v1:
time: 65.7 us; the launch traced here: 65.1 us
  waiting for transfers between devices  27.1 us (41%)
  starting transfers between devices  23.8 us (36%)
  matrix products  10.8 us (16%)
  other arithmetic  2.15 us (3%)
  between operations  0.86 us (1%)
    all_to_all x2, waiting for transfers between devices, shards(): lax.all_to_all(outgoing.reshape(group_size, SLOT_ROWS, LANES), 'grp', spl...  14.6 us
    ppermute x4, starting transfers between devices, passed_along(): return lax.ppermute(block, axis, route)  13.5 us
    ppermute x4, waiting for transfers between devices, passed_along(): return lax.ppermute(block, axis, route)  12.5 us
    all_to_all x2, starting transfers between devices, shards(): lax.all_to_all(outgoing.reshape(group_size, SLOT_ROWS, LANES), 'grp', spl...  10.3 us
    dot_general x2, matrix products, shards(): jnp.einsum('ekij,ei->kej', off_blocks, adjoint_b, preferred_element_type=...  6.55 us
    dot_general x2, matrix products, shards(): outgoing = jnp.dot(place_table, total, precision=lax.Precision.HIGHEST)  2.02 us
    convert_element_type x4, other arithmetic, apply_blocks(): vector.astype(jnp.bfloat16)  1.46 us
  transfers between devices with their start and end apart: 6, of which 6 were waited for; matrix products, arithmetic and copies ran while one was open for 1% of the time, Pallas kernels for 0%

profile of v1, /device:TPU:97, one launch (start us, length us, event | category | flops | bytes accessed | tf_op | source)
XLA Modules:
  0.0 65.1 jit_solution(1662239400631490635)
XLA Ops:
  0.6 0.0 copy-start
  0.6 0.0 copy-start.4
  0.7 0.0 copy-start.3
  0.7 0.0 copy-start.5
  0.7 0.0 copy-start.1
  0.7 0.8 %convert_bitcast_fusion.1 = bf16[12,135,1]{1,0,2:T(8,128)(2,1)S(1)} fusion(f32[12,135]{1,0:T(8,128)} %param.7), kind=kLoop, calls=%fused_computation.43 | loop fusion | flops 1620 | bytes 9720 | tf_op jit(solution)/shard_map/convert_element_type | solution.py:19
  1.5 0.3 copy-done
  1.8 0.0 copy-start.2
  1.8 0.2 fusion.29
  2.0 3.3 %fusion.25 = f32[12,1,6,135]{3,1,2,0:T(1,128)S(1)} fusion(bf16[12,6,135,135]{3,2,1,0:T(8,128)(2,1)} %param.9, bf16[12,135,1,1]{1,0,2,3:T(8,128)(2,1)S(1)} %bitcast.72), kind=kOutput, calls=%fused_computation.34 | convolution fusion | flops 2624400 | bytes 2666520 | tf_op jit(solution)/shard_map/ekij,ei->kej/dot_general | solution.py:44
  5.3 0.0 copy-done.4
  5.4 0.0 copy-done.3
  5.4 0.1 eq.36
  5.5 0.5 fusion.7
  6.0 5.3 %collective-permute-start = (f32[192,256]{1,0:T(8,128)S(1)}, f32[192,256]{1,0:T(8,128)S(1)}, u32[]{:S(2)}, u32[]{:S(2)}) collective-permute-start(f32[192,256]{1,0:T(8,128)S(1)} %get-tuple-element.6), channel_id=1, source_target_pairs={{0,16},{16,32},{32,48},{48,64},{64,80},{80,96},{96,112},{112,128},... | collective-permute-start | bytes 589832 | tf_op jit(solution)/shard_map/ppermute | solution.py:14
  11.4 1.9 %collective-permute-start.1 = (f32[192,256]{1,0:T(8,128)S(1)}, f32[192,256]{1,0:T(8,128)S(1)}, u32[]{:S(2)}, u32[]{:S(2)}) collective-permute-start(f32[192,256]{1,0:T(8,128)S(1)} %get-tuple-element.7), channel_id=1, source_target_pairs={{16,0},{32,16},{48,32},{64,48},{80,64},{96,80},{112,96},{128,112},... | collective-permute-start | bytes 589832 | tf_op jit(solution)/shard_map/ppermute | solution.py:14
  13.3 0.0 copy-done.5
  13.3 0.6 collective-permute-done
  13.9 5.6 %collective-permute-done.1 = f32[192,256]{1,0:T(8,128)S(1)} collective-permute-done((f32[192,256]{1,0:T(8,128)S(1)}, f32[192,256]{1,0:T(8,128)S(1)}, u32[]{:S(2)}, u32[]{:S(2)}) %collective-permute-start.1) | collective-permute-done | bytes 196640 | tf_op jit(solution)/shard_map/ppermute | solution.py:14
  19.6 1.0 %fusion.1 = f32[256,256]{1,0:T(8,128)} fusion(f32[192,256]{1,0:T(8,128)S(1)} %collective-permute-done.1, f32[192,256]{1,0:T(8,128)S(1)} %collective-permute-done, f32[576,256]{1,0:T(8,128)S(1)} %fusion.7, s32[192]{0:T(256)S(1)} %bitcast.74), kind=kOutput, calls=%fused_computation.2 | convolution fusion | flops 151142400 | bytes 852992 | tf_op jit(solution)/shard_map/dot_general | solution.py:54
  20.6 6.8 %all-to-all-start = ((f32[16,16,256]{2,1,0:T(8,128)}), f32[16,16,256]{2,1,0:T(8,128)S(1)}, u32[]{:S(2)}, u32[]{:S(2)}) async-start(f32[16,16,256]{2,1,0:T(8,128)} %bitcast.8), calls=%async_computation | async-start | bytes 524288 | tf_op jit(solution)/shard_map/all_to_all | solution.py:55
  27.3 0.0 copy-done.1
  27.3 0.2 fusion.27
  27.6 7.3 %all-to-all-done = f32[16,16,256]{2,1,0:T(8,128)S(1)} async-done(((f32[16,16,256]{2,1,0:T(8,128)}), f32[16,16,256]{2,1,0:T(8,128)S(1)}, u32[]{:S(2)}, u32[]{:S(2)}) %all-to-all-start) | async-done | bytes 262176 | tf_op jit(solution)/shard_map/all_to_all | solution.py:55
  34.9 0.0 copy-done.2
  34.9 0.2 fusion.23
  35.2 3.3 %fusion.19 = f32[12,1,6,135]{3,1,2,0:T(1,128)S(1)} fusion(bf16[12,6,135,135]{3,2,1,0:T(8,128)(2,1)} %param.9, bf16[12,135,1,1]{1,0,2,3:T(8,128)(2,1)S(1)} %get-tuple-element.9), kind=kOutput, calls=%fused_computation.28 | convolution fusion | flops 2624400 | bytes 2666520 | tf_op jit(solution)/shard_map/ekij,ei->kej/dot_general | solution.py:44
  38.5 0.5 fusion.6
  39.0 4.3 %collective-permute-start.2 = (f32[192,256]{1,0:T(8,128)S(1)}, f32[192,256]{1,0:T(8,128)S(1)}, u32[]{:S(2)}, u32[]{:S(2)}) collective-permute-start(f32[192,256]{1,0:T(8,128)S(1)} %get-tuple-element.4), channel_id=1, source_target_pairs={{0,16},{16,32},{32,48},{48,64},{64,80},{80,96},{96,112},{112,128},... | collective-permute-start | bytes 589832 | tf_op jit(solution)/shard_map/ppermute | solution.py:14
  43.4 1.9 %collective-permute-start.3 = (f32[192,256]{1,0:T(8,128)S(1)}, f32[192,256]{1,0:T(8,128)S(1)}, u32[]{:S(2)}, u32[]{:S(2)}) collective-permute-start(f32[192,256]{1,0:T(8,128)S(1)} %get-tuple-element.5), channel_id=1, source_target_pairs={{16,0},{32,16},{48,32},{64,48},{80,64},{96,80},{112,96},{128,112},... | collective-permute-start | bytes 589832 | tf_op jit(solution)/shard_map/ppermute | solution.py:14
  45.3 0.7 %collective-permute-done.2 = f32[192,256]{1,0:T(8,128)S(1)} collective-permute-done((f32[192,256]{1,0:T(8,128)S(1)}, f32[192,256]{1,0:T(8,128)S(1)}, u32[]{:S(2)}, u32[]{:S(2)}) %collective-permute-start.2) | collective-permute-done | bytes 196640 | tf_op jit(solution)/shard_map/ppermute | solution.py:14
  46.0 5.6 %collective-permute-done.3 = f32[192,256]{1,0:T(8,128)S(1)} collective-permute-done((f32[192,256]{1,0:T(8,128)S(1)}, f32[192,256]{1,0:T(8,128)S(1)}, u32[]{:S(2)}, u32[]{:S(2)}) %collective-permute-start.3) | collective-permute-done | bytes 196640 | tf_op jit(solution)/shard_map/ppermute | solution.py:14
  51.6 1.0 %fusion = f32[256,256]{1,0:T(8,128)} fusion(f32[192,256]{1,0:T(8,128)S(1)} %collective-permute-done.3, f32[192,256]{1,0:T(8,128)S(1)} %collective-permute-done.2, f32[576,256]{1,0:T(8,128)S(1)} %fusion.6, s32[192]{0:T(256)S(1)} %bitcast.75), kind=kOutput, calls=%fused_computation.1 | convolution fusion | flops 151142400 | bytes 852992 | tf_op jit(solution)/shard_map/dot_general | solution.py:54
  52.6 3.5 %all-to-all-start.1 = ((f32[16,16,256]{2,1,0:T(8,128)}), f32[16,16,256]{2,1,0:T(8,128)S(1)}, u32[]{:S(2)}, u32[]{:S(2)}) async-start(f32[16,16,256]{2,1,0:T(8,128)} %bitcast.16), calls=%async_computation.1 | async-start | bytes 524288 | tf_op jit(solution)/shard_map/all_to_all | solution.py:55
  56.1 0.2 fusion.21
  56.3 7.3 %all-to-all-done.1 = f32[16,16,256]{2,1,0:T(8,128)S(1)} async-done(((f32[16,16,256]{2,1,0:T(8,128)}), f32[16,16,256]{2,1,0:T(8,128)S(1)}, u32[]{:S(2)}, u32[]{:S(2)}) %all-to-all-start.1) | async-done | bytes 262176 | tf_op jit(solution)/shard_map/all_to_all | solution.py:55
  63.6 0.6 convert_bitcast_fusion
  64.3 0.2 fusion.17
  64.5 0.6 bitcast_add_fusion
  (13 shorter events, 0.2 us)
Async XLA Ops:
  0.6 1.2 %copy-start = (bf16[12,135,135]{2,1,0:T(8,128)(2,1)S(1)}, bf16[12,135,135]{2,1,0:T(8,128)(2,1)}, u32[]{:S(2)}) copy-start(bf16[12,135,135]{2,1,0:T(8,128)(2,1)} %param.10) | copy-start | bytes 1312204
  0.6 4.7 %copy-start.4 = (s32[6,12]{1,0:T(8,128)S(1)}, s32[6,12]{1,0:T(8,128)}, u32[]{:S(2)}) copy-start(s32[6,12]{1,0:T(8,128)} %param.11) | copy-start | bytes 868
  0.7 4.7 %copy-start.3 = (s32[6,12]{1,0:T(8,128)S(1)}, s32[6,12]{1,0:T(8,128)}, u32[]{:S(2)}) copy-start(s32[6,12]{1,0:T(8,128)} %param.12) | copy-start | bytes 868
  0.7 12.6 %copy-start.5 = (s32[1,192]{1,0:T(1,128)S(1)}, s32[1,192]{1,0:T(1,128)}, u32[]{:S(2)}) copy-start(s32[1,192]{1,0:T(1,128)} %param.13) | copy-start | bytes 2308
  0.7 26.7 %copy-start.1 = (bf16[12,135,135]{2,1,0:T(8,128)(2,1)S(1)}, bf16[12,135,135]{2,1,0:T(8,128)(2,1)}, u32[]{:S(2)}) copy-start(bf16[12,135,135]{2,1,0:T(8,128)(2,1)} %param.8) | copy-start | bytes 1312204
  1.8 33.1 %copy-start.2 = (f32[12,135]{1,0:T(8,128)S(1)}, f32[12,135]{1,0:T(8,128)}, u32[]{:S(2)}) copy-start(f32[12,135]{1,0:T(8,128)} %param.7) | copy-start | bytes 19444
  6.0 7.9 %collective-permute-start = (f32[192,256]{1,0:T(8,128)S(1)}, f32[192,256]{1,0:T(8,128)S(1)}, u32[]{:S(2)}, u32[]{:S(2)}) collective-permute-start(f32[192,256]{1,0:T(8,128)S(1)} %get-tuple-element.6), channel_id=1, source_target_pairs={{0,16},{16,32},{32,48},{48,64},{64,80},{80,96},{96,112},{112,128},... | collective-permute-start | bytes 589832 | tf_op jit(solution)/shard_map/ppermute | solution.py:14
  11.4 8.2 %collective-permute-start.1 = (f32[192,256]{1,0:T(8,128)S(1)}, f32[192,256]{1,0:T(8,128)S(1)}, u32[]{:S(2)}, u32[]{:S(2)}) collective-permute-start(f32[192,256]{1,0:T(8,128)S(1)} %get-tuple-element.7), channel_id=1, source_target_pairs={{16,0},{32,16},{48,32},{64,48},{80,64},{96,80},{112,96},{128,112},... | collective-permute-start | bytes 589832 | tf_op jit(solution)/shard_map/ppermute | solution.py:14
  20.6 14.3 %all-to-all-start = ((f32[16,16,256]{2,1,0:T(8,128)}), f32[16,16,256]{2,1,0:T(8,128)S(1)}, u32[]{:S(2)}, u32[]{:S(2)}) async-start(f32[16,16,256]{2,1,0:T(8,128)} %bitcast.8), calls=%async_computation | async-start | bytes 524288 | tf_op jit(solution)/shard_map/all_to_all | solution.py:55
  39.0 6.9 %collective-permute-start.2 = (f32[192,256]{1,0:T(8,128)S(1)}, f32[192,256]{1,0:T(8,128)S(1)}, u32[]{:S(2)}, u32[]{:S(2)}) collective-permute-start(f32[192,256]{1,0:T(8,128)S(1)} %get-tuple-element.4), channel_id=1, source_target_pairs={{0,16},{16,32},{32,48},{48,64},{64,80},{80,96},{96,112},{112,128},... | collective-permute-start | bytes 589832 | tf_op jit(solution)/shard_map/ppermute | solution.py:14
  43.4 8.2 %collective-permute-start.3 = (f32[192,256]{1,0:T(8,128)S(1)}, f32[192,256]{1,0:T(8,128)S(1)}, u32[]{:S(2)}, u32[]{:S(2)}) collective-permute-start(f32[192,256]{1,0:T(8,128)S(1)} %get-tuple-element.5), channel_id=1, source_target_pairs={{16,0},{32,16},{48,32},{64,48},{80,64},{96,80},{112,96},{128,112},... | collective-permute-start | bytes 589832 | tf_op jit(solution)/shard_map/ppermute | solution.py:14
  52.6 11.0 %all-to-all-start.1 = ((f32[16,16,256]{2,1,0:T(8,128)}), f32[16,16,256]{2,1,0:T(8,128)S(1)}, u32[]{:S(2)}, u32[]{:S(2)}) async-start(f32[16,16,256]{2,1,0:T(8,128)} %bitcast.16), calls=%async_computation.1 | async-start | bytes 524288 | tf_op jit(solution)/shard_map/all_to_all | solution.py:55

commit v2 on v1

v2 whole, which is shorter than its diff:
```python
import jax
import jax.numpy as jnp
from jax import lax
from jax.experimental import pallas as pl
from jax.experimental.pallas import tpu as pltpu
from jax.sharding import PartitionSpec as P

LANES = 128
WIDE = 256
PAD_ROWS = 16
TAIL_STEP = 8
F32 = jnp.float32
BF16 = jnp.bfloat16
PARAMS = pltpu.CompilerParams(vmem_limit_bytes=16 * 1024 * 1024)


def iota(shape, axis):
    return lax.broadcasted_iota(jnp.int32, shape, axis)


def split(values):
    high = values.astype(BF16)
    return high, (values - high.astype(F32)).astype(BF16)


def select_rows(table, values):
    high, low = split(values)
    return jnp.dot(table, high, preferred_element_type=F32) + jnp.dot(
        table, low, preferred_element_type=F32
    )


def block_products(vector_ref, blocks_ref, out_ref):
    elements, width = blocks_ref.shape[0], blocks_ref.shape[-1]
    for e in range(elements):
        row = vector_ref[e : e + 1, 0:width].astype(BF16)
        out_ref[e : e + 1, 0:width] = jnp.dot(row, blocks_ref[e], preferred_element_type=F32)


def face_products(adjoint_ref, blocks_ref, faces_ref, arrived):
    faces_ref[...] = jnp.zeros(faces_ref.shape, F32)
    elements, faces, width = blocks_ref.shape[0], blocks_ref.shape[1], blocks_ref.shape[-1]
    for e in range(elements):
        row = adjoint_ref[e : e + 1, 0:width].astype(BF16)
        arrived(e)
        for k in range(faces):
            at = k * PAD_ROWS + e
            faces_ref[at : at + 1, 0:width] = jnp.dot(
                row, blocks_ref[e, k], preferred_element_type=F32
            )


def face_targets(part_ref, slot_ref, my_part, part_rows):
    faces, elements = part_ref.shape
    part, slot = part_ref[...], slot_ref[...]
    offset = part - my_part
    towards_chip = 1 - 2 * (my_part & 1)
    section = jnp.where(offset == 0, 0, jnp.where(offset == towards_chip, 1, 2))
    target = jnp.where(part < 0, -1, section * part_rows + slot)
    target = jnp.pad(target, ((0, 0), (0, LANES - elements)))
    row = jnp.zeros((1, LANES), jnp.int32)
    lane = iota((1, LANES), 1)
    for k in range(faces):
        moved = pltpu.roll(target[k : k + 1], k * PAD_ROWS, 1)
        row = jnp.where(lane // PAD_ROWS == k, moved, row)
    real = jnp.logical_and(lane < faces * PAD_ROWS, lane % PAD_ROWS < elements)
    return jnp.where(real, row, -1)


def sent_rows(target_row, faces_ref, section, rows):
    count = faces_ref.shape[0]
    table = iota((rows, count), 0) + section * rows == target_row[:, 0:count]
    return select_rows(table.astype(BF16), faces_ref[...])


def first_kernel(
    my_part_ref, forcing_hbm, precond_hbm, off_hbm, diag_hbm, part_hbm, slot_hbm, perm_hbm,
    adjoint_ref, faces_ref, target_ref, next_ref, chip_ref,
    forcing_ref, precond_ref, kept_ref, diag_ref, perm_ref, part_ref, slot_ref, sems, off_sems,
):
    rows = chip_ref.shape[0]
    whole = [
        pltpu.make_async_copy(source, target, sems.at[i])
        for i, (source, target) in enumerate(
            (
                (forcing_hbm, forcing_ref),
                (precond_hbm, precond_ref),
                (part_hbm, part_ref),
                (slot_hbm, slot_ref),
                (perm_hbm, perm_ref),
                (diag_hbm, diag_ref),
            )
        )
    ]
    by_element = [
        pltpu.make_async_copy(off_hbm.at[e], kept_ref.at[e], off_sems.at[e])
        for e in range(off_hbm.shape[0])
    ]
    for copy in whole[:5] + by_element + whole[5:]:
        copy.start()
    adjoint_ref[...] = jnp.zeros(adjoint_ref.shape, F32)
    for copy in whole[:2]:
        copy.wait()
    block_products(forcing_ref, precond_ref, adjoint_ref)
    for copy in whole[2:5]:
        copy.wait()
    target = face_targets(part_ref, slot_ref, my_part_ref[0], rows)
    target_ref[...] = target
    face_products(adjoint_ref, kept_ref, faces_ref, lambda e: by_element[e].wait())
    next_ref[...] = sent_rows(target, faces_ref, 2, rows)
    chip_ref[...] = sent_rows(target, faces_ref, 1, rows)
    whole[5].wait()


def own_part(forcing_ref, adjoint_ref, diag_ref, faces_ref, target_ref, own_ref, rest_ref):
    elements, width = forcing_ref.shape
    own_ref[...] = sent_rows(target_ref[...], faces_ref, 0, own_ref.shape[0])
    rest_ref[...] = jnp.zeros(rest_ref.shape, F32)
    block_products(adjoint_ref, diag_ref, rest_ref)
    rest_ref[0:elements, 0:width] = forcing_ref[...] - rest_ref[0:elements, 0:width]


def own_kernel_first(
    forcing_ref, adjoint_ref, diag_ref, faces_ref, target_ref, perm_ref, own_ref, rest_ref, place_ref
):
    elements = forcing_ref.shape[0]
    perm = perm_ref[...]
    rank = (perm * (65536 // elements + 1)) >> 16
    place = rank * PAD_ROWS + perm - rank * elements
    place_ref[...] = (iota(place_ref.shape, 0) == place).astype(F32).astype(BF16)
    own_part(forcing_ref, adjoint_ref, diag_ref, faces_ref, target_ref, own_ref, rest_ref)


def pack_kernel(own_ref, chip_ref, next_ref, place_ref, out_ref):
    elements_step = TAIL_STEP
    ranks = out_ref.shape[0]
    total = own_ref[...] + chip_ref[...] + next_ref[...]
    placed = select_rows(place_ref[...], total)
    main, tail = placed[:, 0:LANES], placed[:, LANES:WIDE]
    moved = pltpu.roll(tail, 0, 1, stride=elements_step, stride_axis=0)
    row = iota((PAD_ROWS, LANES), 0)
    for r in range(ranks):
        at = slice(r * PAD_ROWS, (r + 1) * PAD_ROWS)
        packed = jnp.sum(moved[at], axis=0, keepdims=True)
        out_ref[r] = jnp.where(row == PAD_ROWS - 4, packed, main[at])


def gathered_rows(arrived_ref, width):
    total = arrived_ref[0]
    for r in range(1, arrived_ref.shape[0]):
        total = total + arrived_ref[r]
    packed = total[PAD_ROWS - 4 : PAD_ROWS - 3]
    tail = jnp.broadcast_to(packed, (PAD_ROWS, LANES))
    row = iota((PAD_ROWS, LANES), 0)
    for r in range(1, PAD_ROWS - 4):
        tail = jnp.where(row == r, pltpu.roll(packed, LANES - TAIL_STEP * r, 1), tail)
    tail = jnp.where(iota((PAD_ROWS, LANES), 1) < width - LANES, tail, 0.0)
    return jnp.concatenate([total, tail], axis=1)


def next_kernel(
    arrived_ref, rest_ref, before_ref, precond_ref, blocks_ref, target_ref,
    adjoint_ref, faces_ref, next_ref, chip_ref, residual_ref,
):
    width = precond_ref.shape[-1]
    rows = chip_ref.shape[0]
    residual_ref[...] = rest_ref[...] - gathered_rows(arrived_ref, width)
    adjoint_ref[...] = jnp.zeros(adjoint_ref.shape, F32)
    block_products(residual_ref, precond_ref, adjoint_ref)
    adjoint_ref[...] = before_ref[...] + adjoint_ref[...]
    face_products(adjoint_ref, blocks_ref, faces_ref, lambda e: None)
    target = target_ref[...]
    next_ref[...] = sent_rows(target, faces_ref, 2, rows)
    chip_ref[...] = sent_rows(target, faces_ref, 1, rows)


def last_kernel(
    arrived_ref, rest_ref, before_ref, precond_ref, adjoint_ref, residual_ref, held_ref, sum_ref
):
    elements, width = residual_ref.shape
    held_ref[...] = rest_ref[...] - gathered_rows(arrived_ref, width)
    residual_ref[...] = held_ref[0:elements, 0:width]
    block_products(held_ref, precond_ref, sum_ref)
    adjoint_ref[...] = before_ref[0:elements, 0:width] + sum_ref[0:elements, 0:width]


def in_hbm(*arrays):
    return [pltpu.with_memory_space_constraint(a, pltpu.HBM) for a in arrays]


def cost(flops):
    return pl.CostEstimate(flops=flops, bytes_accessed=1 << 20, transcendentals=0)


def make_calls(elements, faces, width, ranks):
    part_rows = elements * ranks
    vector = pltpu.VMEM((PAD_ROWS, WIDE), F32)
    sent = pltpu.VMEM((part_rows, WIDE), F32)
    face_rows = pltpu.VMEM((faces * PAD_ROWS, WIDE), F32)
    target = pltpu.VMEM((1, LANES), jnp.int32)
    hbm = pl.BlockSpec(memory_space=pltpu.HBM)
    smem = pl.BlockSpec(memory_space=pltpu.SMEM)
    out = jax.ShapeDtypeStruct((elements, width), F32)
    blocks = pltpu.VMEM((elements, width, width), BF16)
    kept = (
        pltpu.VMEM((elements, width), F32),
        blocks,
        pltpu.VMEM((elements, faces, width, width), BF16),
        blocks,
        pltpu.VMEM((1, part_rows), jnp.int32),
    )
    indices = pltpu.VMEM((faces, elements), jnp.int32)
    first = pl.pallas_call(
        first_kernel,
        out_shape=(vector, face_rows, target, sent, sent, *kept),
        in_specs=[smem] + [hbm] * 7,
        scratch_shapes=[
            indices,
            indices,
            pltpu.SemaphoreType.DMA((6,)),
            pltpu.SemaphoreType.DMA((elements,)),
        ],
        compiler_params=PARAMS,
        name="first",
    )
    own_first = pl.pallas_call(
        own_kernel_first,
        out_shape=(sent, vector, pltpu.VMEM((ranks * PAD_ROWS, part_rows), BF16)),
        compiler_params=PARAMS,
        cost_estimate=cost(10**9),
        name="own_first",
    )
    own_next = pl.pallas_call(
        own_part,
        out_shape=(sent, vector),
        compiler_params=PARAMS,
        cost_estimate=cost(10**9),
        name="own_next",
    )
    pack = pl.pallas_call(
        pack_kernel,
        out_shape=pltpu.VMEM((ranks, PAD_ROWS, LANES), F32),
        compiler_params=PARAMS,
        name="pack",
    )
    following = pl.pallas_call(
        next_kernel,
        out_shape=(vector, face_rows, sent, sent),
        scratch_shapes=[pltpu.VMEM((PAD_ROWS, WIDE), F32)],
        compiler_params=PARAMS,
        name="following",
    )
    last = pl.pallas_call(
        last_kernel,
        out_shape=(out, out),
        scratch_shapes=[pltpu.VMEM((PAD_ROWS, WIDE), F32)] * 2,
        compiler_params=PARAMS,
        name="last",
    )
    return first, own_first, own_next, pack, following, last


def shards(forcing, diag_blocks, off_blocks, precond, face_part, face_slot, row_perm):
    elements, width = forcing.shape
    faces = face_part.shape[0]
    ranks = lax.axis_size("grp")
    parts = lax.axis_size("dom")
    first, own_first, own_next, pack, following, last = make_calls(elements, faces, width, ranks)
    my_part = lax.axis_index("dom").astype(jnp.int32).reshape(1)
    on_chip = [(p, p ^ 1) for p in range(parts)]
    across = [(p, ((p + 1) ^ 1) - 1) for p in range(1, parts - 1)]

    def exchange(beyond, chip):
        from_beyond = lax.ppermute(beyond, "dom", across)
        return from_beyond, lax.ppermute(chip, "dom", on_chip)

    adjoint, face_rows, target, beyond, chip, forcing, precond, kept, diag_blocks, perm = first(
        my_part,
        *in_hbm(forcing, precond, off_blocks, diag_blocks, face_part, face_slot, row_perm),
    )
    from_beyond, from_chip = exchange(beyond, chip)
    own, rest, place = own_first(forcing, adjoint, diag_blocks, face_rows, target, perm)
    arrived = lax.all_to_all(pack(own, from_chip, from_beyond, place), "grp", 0, 0)
    adjoint, face_rows, beyond, chip = following(arrived, rest, adjoint, precond, kept, target)
    from_beyond, from_chip = exchange(beyond, chip)
    own, rest = own_next(forcing, adjoint, diag_blocks, face_rows, target)
    arrived = lax.all_to_all(pack(own, from_chip, from_beyond, place), "grp", 0, 0)
    return last(arrived, rest, adjoint, precond)


def solution(mesh):
    return jax.shard_map(
        shards,
        mesh=mesh,
        in_specs=(
            P(("dom", "grp"), None),
            P(("dom", "grp"), None, None),
            P(("dom", "grp"), None, None, None),
            P(("dom", "grp"), None, None),
            P(None, ("dom", "grp")),
            P(None, ("dom", "grp")),
            P("dom", None),
        ),
        out_specs=(P(("dom", "grp"), None), P(("dom", "grp"), None)),
        check_vma=False,
    )
```

time: 65.7 us -> 59.8 us (0.910)
  the two profiles are of different devices: /device:TPU:97 before, /device:TPU:1 now
where the time goes in v2:
time: 59.8 us; the launch traced here: 59.5 us
  starting transfers between devices  22.9 us (38%)
  blocking collectives  19.1 us (32%)
  Pallas kernels  8.38 us (14%)
  waiting for transfers between devices  8.36 us (14%)
  between operations  0.71 us (1%)
    all_to_all x2, blocking collectives, shards(): lax.all_to_all(pack(own, from_chip, from_beyond, place), 'grp', 0, 0)  19.1 us
    ppermute x2, starting transfers between devices, exchange(): return (from_beyond, lax.ppermute(chip, 'dom', on_chip))  17.9 us
    ppermute x2, waiting for transfers between devices, exchange(): from_beyond = lax.ppermute(beyond, 'dom', across)  8.35 us
    ppermute x2, starting transfers between devices, exchange(): from_beyond = lax.ppermute(beyond, 'dom', across)  4.99 us
    pallas_call x1, Pallas kernels, shards(): first(my_part, *in_hbm(forcing, precond, off_blocks, diag_blocks, face_pa...  4.9 us
    pallas_call x1, Pallas kernels, shards(): following(arrived, rest, adjoint, precond, kept, target)  1.32 us
  transfers between devices with their start and end apart: 4, of which 2 were waited for; matrix products, arithmetic and copies ran while one was open for 0% of the time, Pallas kernels for 1%

profile of v2, /device:TPU:1, one launch (start us, length us, event | category | flops | bytes accessed | tf_op | source)
XLA Modules:
  0.0 59.5 jit_solution(11564244018568976265)
XLA Ops:
  0.6 4.9 %first.1 = (f32[16,256]{1,0:T(8,128)S(1)}, f32[96,256]{1,0:T(8,128)S(1)}, s32[1,128]{1,0:T(1,128)S(1)}, f32[192,256]{1,0:T(8,128)S(1)}, f32[192,256]{1,0:T(8,128...) custom-call(s32[1]{0:T(128)} %bitcast.my_part_ref, ...), custom_call_target="tpu_custom_call" | custom-call | tf_op jit(solution)/shard_map/first/pallas_call | solution.py:277
  5.5 16.0 %collective-permute-start = (f32[192,256]{1,0:T(8,128)S(1)}, f32[192,256]{1,0:T(8,128)S(1)}, u32[]{:S(2)}, u32[]{:S(2)}) collective-permute-start(f32[192,256]{1,0:T(8,128)S(1)} %get-tuple-element.28), channel_id=1, source_target_pairs={{0,16},{16,0},{32,48},{48,32},{64,80},{80,64},{96,112},{112,96},{1... | collective-permute-start | bytes 589832 | tf_op jit(solution)/shard_map/ppermute | solution.py:275
  21.6 1.9 %collective-permute-start.1 = (f32[192,256]{1,0:T(8,128)S(1)}, f32[192,256]{1,0:T(8,128)S(1)}, u32[]{:S(2)}, u32[]{:S(2)}) collective-permute-start(f32[192,256]{1,0:T(8,128)S(1)} %get-tuple-element.29), channel_id=1, source_target_pairs={{16,32},{32,16},{48,64},{64,48},{80,96},{96,80},{112,128},{128,112... | collective-permute-start | bytes 589832 | tf_op jit(solution)/shard_map/ppermute | solution.py:274
  23.5 0.3 own_first.1
  23.8 0.0 collective-permute-done.chip_ref
  23.8 4.8 %collective-permute-done.1.next_ref = f32[192,256]{1,0:T(8,128)S(1)} collective-permute-done((f32[192,256]{1,0:T(8,128)S(1)}, f32[192,256]{1,0:T(8,128)S(1)}, u32[]{:S(2)}, u32[]{:S(2)}) %collective-permute-start.1) | collective-permute-done | bytes 196640 | tf_op jit(solution)/shard_map/ppermute | solution.py:274
  28.6 0.3 pack.2
  28.9 9.4 %all_to_all.10.arrived_ref = f32[16,16,128]{2,1,0:T(8,128)S(1)} all-to-all(f32[16,16,128]{2,1,0:T(8,128)S(1)} %pack.2), channel_id=1, replica_groups=mesh['dom'=64,'grp'=16] {'grp'}, dimensions={0} | all-to-all | bytes 262144 | tf_op jit(solution)/shard_map/all_to_all | solution.py:283
  38.3 1.3 %following.1 = (f32[16,256]{1,0:T(8,128)S(1)}, f32[96,256]{1,0:T(8,128)S(1)}, f32[192,256]{1,0:T(8,128)S(1)}, f32[192,256]{1,0:T(8,128)S(1)}) custom-call(f32[16,16,128]{2,1,0:T(8,128)S(1)} %all_to_all.10.arrived_ref, f32[16,256]{1,0:T(8,128)S(1)} %get-tuple-element.31.rest_ref, f32[16,256]{1,0:T(8,128)S(1)} %get-tuple-element.22.adjoint_ref.before_ref, ...), custom_call_target="tpu_custom_call" | custom-call | tf_op jit(solution)/shard_map/following/pallas_call | solution.py:284
  39.6 1.9 %collective-permute-start.2 = (f32[192,256]{1,0:T(8,128)S(1)}, f32[192,256]{1,0:T(8,128)S(1)}, u32[]{:S(2)}, u32[]{:S(2)}) collective-permute-start(f32[192,256]{1,0:T(8,128)S(1)} %get-tuple-element.37), channel_id=1, source_target_pairs={{0,16},{16,0},{32,48},{48,32},{64,80},{80,64},{96,112},{112,96},{1... | collective-permute-start | bytes 589832 | tf_op jit(solution)/shard_map/ppermute | solution.py:275
  41.6 3.1 %collective-permute-start.3 = (f32[192,256]{1,0:T(8,128)S(1)}, f32[192,256]{1,0:T(8,128)S(1)}, u32[]{:S(2)}, u32[]{:S(2)}) collective-permute-start(f32[192,256]{1,0:T(8,128)S(1)} %get-tuple-element.38), channel_id=1, source_target_pairs={{16,32},{32,16},{48,64},{64,48},{80,96},{96,80},{112,128},{128,112... | collective-permute-start | bytes 589832 | tf_op jit(solution)/shard_map/ppermute | solution.py:274
  44.6 0.3 own_next.1
  44.9 0.0 collective-permute-done.2.chip_ref
  44.9 3.6 %collective-permute-done.3.next_ref = f32[192,256]{1,0:T(8,128)S(1)} collective-permute-done((f32[192,256]{1,0:T(8,128)S(1)}, f32[192,256]{1,0:T(8,128)S(1)}, u32[]{:S(2)}, u32[]{:S(2)}) %collective-permute-start.3) | collective-permute-done | bytes 196640 | tf_op jit(solution)/shard_map/ppermute | solution.py:274
  48.5 0.3 pack.3
  48.9 9.6 %all_to_all.11.arrived_ref = f32[16,16,128]{2,1,0:T(8,128)S(1)} all-to-all(f32[16,16,128]{2,1,0:T(8,128)S(1)} %pack.3), channel_id=1, replica_groups=mesh['dom'=64,'grp'=16] {'grp'}, dimensions={0} | all-to-all | bytes 262144 | tf_op jit(solution)/shard_map/all_to_all | solution.py:287
  58.5 0.9 %last.1 = (f32[12,135]{1,0:T(8,128)}, f32[12,135]{1,0:T(8,128)}) custom-call(f32[16,16,128]{2,1,0:T(8,128)S(1)} %all_to_all.11.arrived_ref, f32[16,256]{1,0:T(8,128)S(1)} %get-tuple-element.39.rest_ref, f32[16,256]{1,0:T(8,128)S(1)} %get-tuple-element.34.adjoint_ref.before_ref, bf16[12,135,135]{2,1,0:T(8,128)(2,1)S(1)} %get-tuple-element.32.precond_ref), custom_call_target="tpu_custom_call" | custom-call | tf_op jit(solution)/shard_map/last/pallas_call | solution.py:288
Async XLA Ops:
  5.5 18.3 %collective-permute-start = (f32[192,256]{1,0:T(8,128)S(1)}, f32[192,256]{1,0:T(8,128)S(1)}, u32[]{:S(2)}, u32[]{:S(2)}) collective-permute-start(f32[192,256]{1,0:T(8,128)S(1)} %get-tuple-element.28), channel_id=1, source_target_pairs={{0,16},{16,0},{32,48},{48,32},{64,80},{80,64},{96,112},{112,96},{1... | collective-permute-start | bytes 589832 | tf_op jit(solution)/shard_map/ppermute | solution.py:275
  21.6 7.0 %collective-permute-start.1 = (f32[192,256]{1,0:T(8,128)S(1)}, f32[192,256]{1,0:T(8,128)S(1)}, u32[]{:S(2)}, u32[]{:S(2)}) collective-permute-start(f32[192,256]{1,0:T(8,128)S(1)} %get-tuple-element.29), channel_id=1, source_target_pairs={{16,32},{32,16},{48,64},{64,48},{80,96},{96,80},{112,128},{128,112... | collective-permute-start | bytes 589832 | tf_op jit(solution)/shard_map/ppermute | solution.py:274
  39.6 5.3 %collective-permute-start.2 = (f32[192,256]{1,0:T(8,128)S(1)}, f32[192,256]{1,0:T(8,128)S(1)}, u32[]{:S(2)}, u32[]{:S(2)}) collective-permute-start(f32[192,256]{1,0:T(8,128)S(1)} %get-tuple-element.37), channel_id=1, source_target_pairs={{0,16},{16,0},{32,48},{48,32},{64,80},{80,64},{96,112},{112,96},{1... | collective-permute-start | bytes 589832 | tf_op jit(solution)/shard_map/ppermute | solution.py:275
  41.6 7.0 %collective-permute-start.3 = (f32[192,256]{1,0:T(8,128)S(1)}, f32[192,256]{1,0:T(8,128)S(1)}, u32[]{:S(2)}, u32[]{:S(2)}) collective-permute-start(f32[192,256]{1,0:T(8,128)S(1)} %get-tuple-element.38), channel_id=1, source_target_pairs={{16,32},{32,16},{48,64},{64,48},{80,96},{96,80},{112,128},{128,112... | collective-permute-start | bytes 589832 | tf_op jit(solution)/shard_map/ppermute | solution.py:274

commit v3 on v2

--- a/solution.py
+++ b/solution.py
@@ -1,3 +1,5 @@
+import functools
+
 import jax
 import jax.numpy as jnp
 from jax import lax
@@ -67,18 +69,32 @@
     return jnp.where(real, row, -1)
 
 
-def sent_rows(target_row, faces_ref, section, rows):
+def contract(left, right):
+    return lax.dot_general(left, right, (((1,), (1,)), ((), ())), preferred_element_type=F32)
+
+
+def store_sent(target_row, faces_ref, tails_ref, section, out_ref):
     count = faces_ref.shape[0]
-    table = iota((rows, count), 0) + section * rows == target_row[:, 0:count]
-    return select_rows(table.astype(BF16), faces_ref[...])
+    rows = out_ref.shape[0] - PAD_ROWS
+    table = (iota((rows, count), 0) + section * rows == target_row[:, 0:count]).astype(BF16)
+    out_ref[0:rows] = select_rows(table, faces_ref[:, 0:LANES])
+    high, low = split(tails_ref[...])
+    tails = contract(high[:, 0:count], table) + contract(low[:, 0:count], table)
+    out_ref[rows : rows + TAIL_STEP] = tails[:, 0:LANES]
+    out_ref[rows + TAIL_STEP :] = jnp.pad(tails[:, LANES:], ((0, 0), (0, WIDE - rows)))
+
+
+def store_tails(faces_ref, tails_ref):
+    tail = jnp.pad(faces_ref[:, LANES:WIDE], ((0, LANES - faces_ref.shape[0]), (0, 0)))
+    tails_ref[...] = jnp.transpose(tail)[0:TAIL_STEP]
 
 
 def first_kernel(
-    my_part_ref, forcing_hbm, precond_hbm, off_hbm, diag_hbm, part_hbm, slot_hbm, perm_hbm,
-    adjoint_ref, faces_ref, target_ref, next_ref, chip_ref,
-    forcing_ref, precond_ref, kept_ref, diag_ref, perm_ref, part_ref, slot_ref, sems, off_sems,
-):
-    rows = chip_ref.shape[0]
+    ahead, my_part_ref, forcing_hbm, precond_hbm, off_hbm, part_hbm, slot_hbm,
+    adjoint_ref, faces_ref, tails_ref, target_ref, next_ref,
+    forcing_ref, precond_ref, kept_ref, part_ref, slot_ref, sems, off_sems,
+):
+    rows = next_ref.shape[0] - PAD_ROWS
     whole = [
         pltpu.make_async_copy(source, target, sems.at[i])
         for i, (source, target) in enumerate(
@@ -87,8 +103,6 @@
                 (precond_hbm, precond_ref),
                 (part_hbm, part_ref),
                 (slot_hbm, slot_ref),
-                (perm_hbm, perm_ref),
-                (diag_hbm, diag_ref),
             )
         )
     ]
@@ -96,48 +110,80 @@
         pltpu.make_async_copy(off_hbm.at[e], kept_ref.at[e], off_sems.at[e])
         for e in range(off_hbm.shape[0])
     ]
-    for copy in whole[:5] + by_element + whole[5:]:
+    for copy in whole + by_element[:ahead]:
         copy.start()
     adjoint_ref[...] = jnp.zeros(adjoint_ref.shape, F32)
-    for copy in whole[:2]:
-        copy.wait()
-    block_products(forcing_ref, precond_ref, adjoint_ref)
-    for copy in whole[2:5]:
+    for copy in whole:
         copy.wait()
     target = face_targets(part_ref, slot_ref, my_part_ref[0], rows)
     target_ref[...] = target
-    face_products(adjoint_ref, kept_ref, faces_ref, lambda e: by_element[e].wait())
-    next_ref[...] = sent_rows(target, faces_ref, 2, rows)
-    chip_ref[...] = sent_rows(target, faces_ref, 1, rows)
-    whole[5].wait()
-
-
-def own_part(forcing_ref, adjoint_ref, diag_ref, faces_ref, target_ref, own_ref, rest_ref):
+    block_products(forcing_ref, precond_ref, adjoint_ref)
+
+    def arrived(e):
+        if e + ahead < len(by_element):
+            by_element[e + ahead].start()
+        by_element[e].wait()
+
+    face_products(adjoint_ref, kept_ref, faces_ref, arrived)
+    store_tails(faces_ref, tails_ref)
+    store_sent(target, faces_ref, tails_ref, 2, next_ref)
+
+
+def chip_kernel(faces_ref, tails_ref, target_ref, chip_ref):
+    store_sent(target_ref[...], faces_ref, tails_ref, 1, chip_ref)
+
+
+def own_part(
+    forcing_ref, adjoint_ref, diag_ref, faces_ref, tails_ref, target_ref, own_ref, rest_ref, arrived
+):
     elements, width = forcing_ref.shape
-    own_ref[...] = sent_rows(target_ref[...], faces_ref, 0, own_ref.shape[0])
+    store_sent(target_ref[...], faces_ref, tails_ref, 0, own_ref)
     rest_ref[...] = jnp.zeros(rest_ref.shape, F32)
+    arrived()
     block_products(adjoint_ref, diag_ref, rest_ref)
     rest_ref[0:elements, 0:width] = forcing_ref[...] - rest_ref[0:elements, 0:width]
 
 
 def own_kernel_first(
-    forcing_ref, adjoint_ref, diag_ref, faces_ref, target_ref, perm_ref, own_ref, rest_ref, place_ref
-):
+    forcing_ref, adjoint_ref, diag_hbm, faces_ref, tails_ref, target_ref, perm_hbm,
+    own_ref, rest_ref, place_ref, diag_ref, perm_ref, sems,
+):
+    copies = [
+        pltpu.make_async_copy(perm_hbm, perm_ref, sems.at[0]),
+        pltpu.make_async_copy(diag_hbm, diag_ref, sems.at[1]),
+    ]
+    for copy in copies:
+        copy.start()
+    own_part(
+        forcing_ref, adjoint_ref, diag_ref, faces_ref, tails_ref, target_ref, own_ref, rest_ref,
+        lambda: [copy.wait() for copy in copies],
+    )
     elements = forcing_ref.shape[0]
     perm = perm_ref[...]
     rank = (perm * (65536 // elements + 1)) >> 16
     place = rank * PAD_ROWS + perm - rank * elements
     place_ref[...] = (iota(place_ref.shape, 0) == place).astype(F32).astype(BF16)
-    own_part(forcing_ref, adjoint_ref, diag_ref, faces_ref, target_ref, own_ref, rest_ref)
+
+
+def own_kernel_next(
+    forcing_ref, adjoint_ref, diag_ref, faces_ref, tails_ref, target_ref, own_ref, rest_ref
+):
+    own_part(
+        forcing_ref, adjoint_ref, diag_ref, faces_ref, tails_ref, target_ref, own_ref, rest_ref,
+        lambda: None,
+    )
 
 
 def pack_kernel(own_ref, chip_ref, next_ref, place_ref, out_ref):
-    elements_step = TAIL_STEP
     ranks = out_ref.shape[0]
+    rows = own_ref.shape[0] - PAD_ROWS
     total = own_ref[...] + chip_ref[...] + next_ref[...]
-    placed = select_rows(place_ref[...], total)
-    main, tail = placed[:, 0:LANES], placed[:, LANES:WIDE]
-    moved = pltpu.roll(tail, 0, 1, stride=elements_step, stride_axis=0)
+    place = place_ref[...]
+    main = select_rows(place, total[0:rows])
+    tails = jnp.concatenate([total[rows : rows + TAIL_STEP], total[rows + TAIL_STEP :]], axis=1)
+    high, low = split(jnp.pad(tails[:, 0:rows], ((0, LANES - TAIL_STEP), (0, 0))))
+    tail = contract(place, high) + contract(place, low)
+    moved = pltpu.roll(tail, 0, 1, stride=TAIL_STEP, stride_axis=0)
     row = iota((PAD_ROWS, LANES), 0)
     for r in range(ranks):
         at = slice(r * PAD_ROWS, (r + 1) * PAD_ROWS)
@@ -160,18 +206,16 @@
 
 def next_kernel(
     arrived_ref, rest_ref, before_ref, precond_ref, blocks_ref, target_ref,
-    adjoint_ref, faces_ref, next_ref, chip_ref, residual_ref,
+    adjoint_ref, faces_ref, tails_ref, next_ref, residual_ref,
 ):
     width = precond_ref.shape[-1]
-    rows = chip_ref.shape[0]
     residual_ref[...] = rest_ref[...] - gathered_rows(arrived_ref, width)
     adjoint_ref[...] = jnp.zeros(adjoint_ref.shape, F32)
     block_products(residual_ref, precond_ref, adjoint_ref)
     adjoint_ref[...] = before_ref[...] + adjoint_ref[...]
     face_products(adjoint_ref, blocks_ref, faces_ref, lambda e: None)
-    target = target_ref[...]
-    next_ref[...] = sent_rows(target, faces_ref, 2, rows)
-    chip_ref[...] = sent_rows(target, faces_ref, 1, rows)
+    store_tails(faces_ref, tails_ref)
+    store_sent(target_ref[...], faces_ref, tails_ref, 2, next_ref)
 
 
 def last_kernel(
@@ -192,46 +236,54 @@
     return pl.CostEstimate(flops=flops, bytes_accessed=1 << 20, transcendentals=0)
 
 
-def make_calls(elements, faces, width, ranks):
+def make_calls(elements, faces, width, ranks, ahead=6):
     part_rows = elements * ranks
     vector = pltpu.VMEM((PAD_ROWS, WIDE), F32)
-    sent = pltpu.VMEM((part_rows, WIDE), F32)
+    sent = pltpu.VMEM((part_rows + PAD_ROWS, LANES), F32)
     face_rows = pltpu.VMEM((faces * PAD_ROWS, WIDE), F32)
+    tails = pltpu.VMEM((TAIL_STEP, LANES), F32)
     target = pltpu.VMEM((1, LANES), jnp.int32)
     hbm = pl.BlockSpec(memory_space=pltpu.HBM)
     smem = pl.BlockSpec(memory_space=pltpu.SMEM)
+    vmem = pl.BlockSpec(memory_space=pltpu.VMEM)
     out = jax.ShapeDtypeStruct((elements, width), F32)
     blocks = pltpu.VMEM((elements, width, width), BF16)
     kept = (
         pltpu.VMEM((elements, width), F32),
         blocks,
         pltpu.VMEM((elements, faces, width, width), BF16),
-        blocks,
-        pltpu.VMEM((1, part_rows), jnp.int32),
     )
     indices = pltpu.VMEM((faces, elements), jnp.int32)
     first = pl.pallas_call(
-        first_kernel,
-        out_shape=(vector, face_rows, target, sent, sent, *kept),
-        in_specs=[smem] + [hbm] * 7,
+        functools.partial(first_kernel, ahead),
+        out_shape=(vector, face_rows, tails, target, sent, *kept),
+        in_specs=[smem] + [hbm] * 5,
         scratch_shapes=[
             indices,
             indices,
-            pltpu.SemaphoreType.DMA((6,)),
+            pltpu.SemaphoreType.DMA((4,)),
             pltpu.SemaphoreType.DMA((elements,)),
         ],
         compiler_params=PARAMS,
         name="first",
     )
+    chip = pl.pallas_call(
+        chip_kernel,
+        out_shape=sent,
+        compiler_params=PARAMS,
+        name="chip",
+    )
     own_first = pl.pallas_call(
         own_kernel_first,
-        out_shape=(sent, vector, pltpu.VMEM((ranks * PAD_ROWS, part_rows), BF16)),
+        out_shape=(sent, vector, pltpu.VMEM((ranks * PAD_ROWS, part_rows), BF16), blocks),
+        in_specs=[vmem, vmem, hbm, vmem, vmem, vmem, hbm],
+        scratch_shapes=[pltpu.VMEM((1, part_rows), jnp.int32), pltpu.SemaphoreType.DMA((2,))],
         compiler_params=PARAMS,
         cost_estimate=cost(10**9),
         name="own_first",
     )
     own_next = pl.pallas_call(
-        own_part,
+        own_kernel_next,
         out_shape=(sent, vector),
         compiler_params=PARAMS,
         cost_estimate=cost(10**9),
@@ -245,19 +297,19 @@
     )
     following = pl.pallas_call(
         next_kernel,
-        out_shape=(vector, face_rows, sent, sent),
-        scratch_shapes=[pltpu.VMEM((PAD_ROWS, WIDE), F32)],
+        out_shape=(vector, face_rows, tails, sent),
+        scratch_shapes=[vector],
         compiler_params=PARAMS,
         name="following",
     )
     last = pl.pallas_call(
         last_kernel,
         out_shape=(out, out),
-        scratch_shapes=[pltpu.VMEM((PAD_ROWS, WIDE), F32)] * 2,
+        scratch_shapes=[vector] * 2,
         compiler_params=PARAMS,
         name="last",
     )
-    return first, own_first, own_next, pack, following, last
+    return first, chip, own_first, own_next, pack, following, last
 
 
 def shards(forcing, diag_blocks, off_blocks, precond, face_part, face_slot, row_perm):
@@ -265,25 +317,33 @@
     faces = face_part.shape[0]
     ranks = lax.axis_size("grp")
     parts = lax.axis_size("dom")
-    first, own_first, own_next, pack, following, last = make_calls(elements, faces, width, ranks)
+    first, chip, own_first, own_next, pack, following, last = make_calls(
+        elements, faces, width, ranks
+    )
     my_part = lax.axis_index("dom").astype(jnp.int32).reshape(1)
     on_chip = [(p, p ^ 1) for p in range(parts)]
     across = [(p, ((p + 1) ^ 1) - 1) for p in range(1, parts - 1)]
-
-    def exchange(beyond, chip):
+    forcing, precond, off_blocks, diag_blocks, face_part, face_slot, row_perm = in_hbm(
+        forcing, precond, off_blocks, diag_blocks, face_part, face_slot, row_perm
+    )
+
+    def exchange(beyond, face_terms):
         from_beyond = lax.ppermute(beyond, "dom", across)
-        return from_beyond, lax.ppermute(chip, "dom", on_chip)
-
-    adjoint, face_rows, target, beyond, chip, forcing, precond, kept, diag_blocks, perm = first(
-        my_part,
-        *in_hbm(forcing, precond, off_blocks, diag_blocks, face_part, face_slot, row_perm),
-    )
-    from_beyond, from_chip = exchange(beyond, chip)
-    own, rest, place = own_first(forcing, adjoint, diag_blocks, face_rows, target, perm)
+        sent = chip(*face_terms, target)
+        return from_beyond, lax.ppermute(sent, "dom", on_chip)
+
+    adjoint, *face_terms, target, beyond, forcing, precond, kept = first(
+        my_part, forcing, precond, off_blocks, face_part, face_slot
+    )
+    from_beyond, from_chip = exchange(beyond, face_terms)
+    own, rest, place, diag_blocks = own_first(
+        forcing, adjoint, diag_blocks, *face_terms, target, row_perm
+    )
     arrived = lax.all_to_all(pack(own, from_chip, from_beyond, place), "grp", 0, 0)
-    adjoint, face_rows, beyond, chip = following(arrived, rest, adjoint, precond, kept, target)
-    from_beyond, from_chip = exchange(beyond, chip)
-    own, rest = own_next(forcing, adjoint, diag_blocks, face_rows, target)
+
+    adjoint, *face_terms, beyond = following(arrived, rest, adjoint, precond, kept, target)
+    from_beyond, from_chip = exchange(beyond, face_terms)
+    own, rest = own_next(forcing, adjoint, diag_blocks, *face_terms, target)
     arrived = lax.all_to_all(pack(own, from_chip, from_beyond, place), "grp", 0, 0)
     return last(arrived, rest, adjoint, precond)
 

time: 59.8 us -> 57.8 us (0.967)
  waiting for transfers between devices: 8.36 us -> 5.22 us
  Pallas kernels: 8.38 us -> 9.54 us
    ppermute x2, waiting for transfers between devices: 8.35 us -> 5.21 us  [exchange(): from_beyond = lax.ppermute(beyond, 'dom', across)]
    pallas_call x3 -> x5, Pallas kernels: 5.5 us -> 6.53 us  [the longest x1 4.34 us: shards(): first(my_part, forcing, precond, off_blocks, face_part, face_slot)]
  transfers between devices with their start and end apart: 4 -> 4, of which waited for: 2 -> 2; matrix products, arithmetic and copies ran while one was open for 0% -> 0% of each run, Pallas kernels for 1% -> 3%
where the time goes in v3:
time: 57.8 us; the launch traced here: 57.5 us
  starting transfers between devices  22.9 us (40%)
  blocking collectives  19.1 us (33%)
  Pallas kernels  9.54 us (17%)
  waiting for transfers between devices  5.22 us (9%)
  between operations  0.71 us (1%)
    all_to_all x2, blocking collectives, shards(): lax.all_to_all(pack(own, from_chip, from_beyond, place), 'grp', 0, 0)  19.1 us
    ppermute x2, starting transfers between devices, exchange(): return (from_beyond, lax.ppermute(sent, 'dom', on_chip))  17.9 us
    ppermute x2, waiting for transfers between devices, exchange(): from_beyond = lax.ppermute(beyond, 'dom', across)  5.21 us
    ppermute x2, starting transfers between devices, exchange(): from_beyond = lax.ppermute(beyond, 'dom', across)  4.99 us
    pallas_call x1, Pallas kernels, shards(): first(my_part, forcing, precond, off_blocks, face_part, face_slot)  4.34 us
    pallas_call x1, Pallas kernels, shards(): own_first(forcing, adjoint, diag_blocks, *face_terms, target, row_perm)  1.48 us
    pallas_call x1, Pallas kernels, shards(): following(arrived, rest, adjoint, precond, kept, target)  1.32 us
  transfers between devices with their start and end apart: 4, of which 2 were waited for; matrix products, arithmetic and copies ran while one was open for 0% of the time, Pallas kernels for 3%

profile of v3, /device:TPU:1, one launch (start us, length us, event | category | flops | bytes accessed | tf_op | source)
XLA Modules:
  0.0 57.5 jit_solution(4554479889537858516)
XLA Ops:
  0.6 4.3 %first.1 = (f32[16,256]{1,0:T(8,128)S(1)}, f32[96,256]{1,0:T(8,128)S(1)}, f32[8,128]{1,0:T(8,128)S(1)}, s32[1,128]{1,0:T(1,128)S(1)}, f32[208,128]{1,0:T(8,128)S...) custom-call(s32[1]{0:T(128)} %bitcast.my_part_ref, ...), custom_call_target="tpu_custom_call" | custom-call | tf_op jit(solution)/shard_map/first/pallas_call | solution.py:335
  5.0 0.2 chip.2
  5.2 16.0 %collective-permute-start = (f32[208,128]{1,0:T(8,128)S(1)}, f32[208,128]{1,0:T(8,128)S(1)}, u32[]{:S(2)}, u32[]{:S(2)}) collective-permute-start(f32[208,128]{1,0:T(8,128)S(1)} %chip.2), channel_id=1, source_target_pairs={{0,16},{16,0},{32,48},{48,32},{64,80},{80,64},{96,112},{112,96},{1... | collective-permute-start | bytes 319496 | tf_op jit(solution)/shard_map/ppermute | solution.py:333
  21.2 1.9 %collective-permute-start.1 = (f32[208,128]{1,0:T(8,128)S(1)}, f32[208,128]{1,0:T(8,128)S(1)}, u32[]{:S(2)}, u32[]{:S(2)}) collective-permute-start(f32[208,128]{1,0:T(8,128)S(1)} %get-tuple-element.26), channel_id=1, source_target_pairs={{16,32},{32,16},{48,64},{64,48},{80,96},{96,80},{112,128},{128,112... | collective-permute-start | bytes 319496 | tf_op jit(solution)/shard_map/ppermute | solution.py:331
  23.1 1.5 %own_first.1 = (f32[208,128]{1,0:T(8,128)S(1)}, f32[16,256]{1,0:T(8,128)S(1)}, bf16[256,192]{1,0:T(8,128)(2,1)S(1)}, bf16[12,135,135]{2,1,0:T(8,128)(2,1)S(1)}) custom-call(f32[12,135]{1,0:T(8,128)S(1)} %get-tuple-element.20.forcing_ref, f32[16,256]{1,0:T(8,128)S(1)} %get-tuple-element.21.adjoint_ref.before_ref, bf16[12,135,135]{2,1,0:T(8,128)(2,1)} %diag_hbm.1, ...), custom_call_target="tpu_custom_call" | custom-call | flops 1000000000 | bytes 1048576 | tf_op jit(solution)/shard_map/own_first/pallas_call | solution.py:339
  24.6 0.0 collective-permute-done.chip_ref
  24.6 2.6 %collective-permute-done.1.next_ref = f32[208,128]{1,0:T(8,128)S(1)} collective-permute-done((f32[208,128]{1,0:T(8,128)S(1)}, f32[208,128]{1,0:T(8,128)S(1)}, u32[]{:S(2)}, u32[]{:S(2)}) %collective-permute-start.1) | collective-permute-done | bytes 106528 | tf_op jit(solution)/shard_map/ppermute | solution.py:331
  27.2 0.4 pack.2
  27.6 9.4 %all_to_all.10.arrived_ref = f32[16,16,128]{2,1,0:T(8,128)S(1)} all-to-all(f32[16,16,128]{2,1,0:T(8,128)S(1)} %pack.2), channel_id=1, replica_groups=mesh['dom'=64,'grp'=16] {'grp'}, dimensions={0} | all-to-all | bytes 262144 | tf_op jit(solution)/shard_map/all_to_all | solution.py:342
  37.0 1.3 %following.1 = (f32[16,256]{1,0:T(8,128)S(1)}, f32[96,256]{1,0:T(8,128)S(1)}, f32[8,128]{1,0:T(8,128)S(1)}, f32[208,128]{1,0:T(8,128)S(1)}) custom-call(f32[16,16,128]{2,1,0:T(8,128)S(1)} %all_to_all.10.arrived_ref, f32[16,256]{1,0:T(8,128)S(1)} %get-tuple-element.28.rest_ref, f32[16,256]{1,0:T(8,128)S(1)} %get-tuple-element.21.adjoint_ref.before_ref, ...), custom_call_target="tpu_custom_call" | custom-call | tf_op jit(solution)/shard_map/following/pallas_call | solution.py:344
  38.4 0.2 chip.3
  38.6 1.9 %collective-permute-start.2 = (f32[208,128]{1,0:T(8,128)S(1)}, f32[208,128]{1,0:T(8,128)S(1)}, u32[]{:S(2)}, u32[]{:S(2)}) collective-permute-start(f32[208,128]{1,0:T(8,128)S(1)} %chip.3), channel_id=1, source_target_pairs={{0,16},{16,0},{32,48},{48,32},{64,80},{80,64},{96,112},{112,96},{1... | collective-permute-start | bytes 319496 | tf_op jit(solution)/shard_map/ppermute | solution.py:333
  40.5 3.1 %collective-permute-start.3 = (f32[208,128]{1,0:T(8,128)S(1)}, f32[208,128]{1,0:T(8,128)S(1)}, u32[]{:S(2)}, u32[]{:S(2)}) collective-permute-start(f32[208,128]{1,0:T(8,128)S(1)} %get-tuple-element.36), channel_id=1, source_target_pairs={{16,32},{32,16},{48,64},{64,48},{80,96},{96,80},{112,128},{128,112... | collective-permute-start | bytes 319496 | tf_op jit(solution)/shard_map/ppermute | solution.py:331
  43.6 0.3 own_next.1
  43.9 0.0 collective-permute-done.2.chip_ref
  43.9 2.6 %collective-permute-done.3.next_ref = f32[208,128]{1,0:T(8,128)S(1)} collective-permute-done((f32[208,128]{1,0:T(8,128)S(1)}, f32[208,128]{1,0:T(8,128)S(1)}, u32[]{:S(2)}, u32[]{:S(2)}) %collective-permute-start.3) | collective-permute-done | bytes 106528 | tf_op jit(solution)/shard_map/ppermute | solution.py:331
  46.5 0.4 pack.3
  46.9 9.6 %all_to_all.11.arrived_ref = f32[16,16,128]{2,1,0:T(8,128)S(1)} all-to-all(f32[16,16,128]{2,1,0:T(8,128)S(1)} %pack.3), channel_id=1, replica_groups=mesh['dom'=64,'grp'=16] {'grp'}, dimensions={0} | all-to-all | bytes 262144 | tf_op jit(solution)/shard_map/all_to_all | solution.py:347
  56.5 0.9 %last.1 = (f32[12,135]{1,0:T(8,128)}, f32[12,135]{1,0:T(8,128)}) custom-call(f32[16,16,128]{2,1,0:T(8,128)S(1)} %all_to_all.11.arrived_ref, f32[16,256]{1,0:T(8,128)S(1)} %get-tuple-element.37.rest_ref, f32[16,256]{1,0:T(8,128)S(1)} %get-tuple-element.31.adjoint_ref.before_ref, bf16[12,135,135]{2,1,0:T(8,128)(2,1)S(1)} %get-tuple-element.29.precond_ref), custom_call_target="tpu_custom_call" | custom-call | tf_op jit(solution)/shard_map/last/pallas_call | solution.py:348
Async XLA Ops:
  5.2 19.4 %collective-permute-start = (f32[208,128]{1,0:T(8,128)S(1)}, f32[208,128]{1,0:T(8,128)S(1)}, u32[]{:S(2)}, u32[]{:S(2)}) collective-permute-start(f32[208,128]{1,0:T(8,128)S(1)} %chip.2), channel_id=1, source_target_pairs={{0,16},{16,0},{32,48},{48,32},{64,80},{80,64},{96,112},{112,96},{1... | collective-permute-start | bytes 319496 | tf_op jit(solution)/shard_map/ppermute | solution.py:333
  21.2 6.0 %collective-permute-start.1 = (f32[208,128]{1,0:T(8,128)S(1)}, f32[208,128]{1,0:T(8,128)S(1)}, u32[]{:S(2)}, u32[]{:S(2)}) collective-permute-start(f32[208,128]{1,0:T(8,128)S(1)} %get-tuple-element.26), channel_id=1, source_target_pairs={{16,32},{32,16},{48,64},{64,48},{80,96},{96,80},{112,128},{128,112... | collective-permute-start | bytes 319496 | tf_op jit(solution)/shard_map/ppermute | solution.py:331
  38.6 5.3 %collective-permute-start.2 = (f32[208,128]{1,0:T(8,128)S(1)}, f32[208,128]{1,0:T(8,128)S(1)}, u32[]{:S(2)}, u32[]{:S(2)}) collective-permute-start(f32[208,128]{1,0:T(8,128)S(1)} %chip.3), channel_id=1, source_target_pairs={{0,16},{16,0},{32,48},{48,32},{64,80},{80,64},{96,112},{112,96},{1... | collective-permute-start | bytes 319496 | tf_op jit(solution)/shard_map/ppermute | solution.py:333
  40.5 6.0 %collective-permute-start.3 = (f32[208,128]{1,0:T(8,128)S(1)}, f32[208,128]{1,0:T(8,128)S(1)}, u32[]{:S(2)}, u32[]{:S(2)}) collective-permute-start(f32[208,128]{1,0:T(8,128)S(1)} %get-tuple-element.36), channel_id=1, source_target_pairs={{16,32},{32,16},{48,64},{64,48},{80,96},{96,80},{112,128},{128,112... | collective-permute-start | bytes 319496 | tf_op jit(solution)/shard_map/ppermute | solution.py:331

commit v4 on v2

v4 whole, which is shorter than its diff:
```python
import functools

import jax
import jax.numpy as jnp
from jax import lax
from jax.experimental import pallas as pl
from jax.experimental.pallas import tpu as pltpu
from jax.sharding import PartitionSpec as P

LANES = 128
WIDE = 256
PAD_ROWS = 16
TAIL_STEP = 8
F32 = jnp.float32
BF16 = jnp.bfloat16
PARAMS = pltpu.CompilerParams(vmem_limit_bytes=16 * 1024 * 1024)


def iota(shape, axis):
    return lax.broadcasted_iota(jnp.int32, shape, axis)


def split(values):
    high = values.astype(BF16)
    return high, (values - high.astype(F32)).astype(BF16)


def contract(left, right):
    return lax.dot_general(left, right, (((1,), (1,)), ((), ())), preferred_element_type=F32)


def block_products(vector_ref, blocks_ref, out_ref):
    elements, width = blocks_ref.shape[0], blocks_ref.shape[-1]
    for e in range(elements):
        row = vector_ref[e : e + 1, 0:width].astype(BF16)
        out_ref[e : e + 1, 0:width] = jnp.dot(row, blocks_ref[e], preferred_element_type=F32)


def face_products(adjoint_ref, blocks_ref, sent_ref, tails_ref, arrived):
    elements, faces, width = blocks_ref.shape[0], blocks_ref.shape[1], blocks_ref.shape[-1]
    tails_ref[...] = jnp.zeros(tails_ref.shape, F32)
    for e in range(elements):
        row = adjoint_ref[e : e + 1, 0:width].astype(BF16)
        arrived(e)
        for k in range(faces):
            at = k * elements + e
            product = jnp.dot(row, blocks_ref[e, k], preferred_element_type=F32)
            sent_ref[at : at + 1, :] = product[:, 0:LANES]
            tails_ref[at : at + 1, 0 : width - LANES] = product[:, LANES:width]
    count = faces * elements
    sent_ref[count : count + TAIL_STEP, :] = jnp.transpose(tails_ref[...])[0:TAIL_STEP]


def face_targets(part_ref, slot_ref, my_part, part_rows):
    faces, elements = part_ref.shape
    part, slot = part_ref[...], slot_ref[...]
    offset = part - my_part
    towards_chip = 1 - 2 * (my_part & 1)
    section = jnp.where(offset == 0, 0, jnp.where(offset == towards_chip, 1, 2))
    target = jnp.where(part < 0, -1, section * part_rows + slot)
    target = jnp.pad(target, ((0, 0), (0, LANES - elements)))
    row = jnp.full((1, LANES), -1, jnp.int32)
    lane = iota((1, LANES), 1)
    for k in range(faces):
        moved = pltpu.roll(target[k : k + 1], k * elements, 1)
        inside = jnp.logical_and(lane >= k * elements, lane < (k + 1) * elements)
        row = jnp.where(inside, moved, row)
    return row


def store_target(target_row, sent_ref, count):
    row = jnp.broadcast_to(target_row.astype(F32), (TAIL_STEP, LANES))
    sent_ref[count + TAIL_STEP :, :] = row


def first_kernel(
    ahead, my_part_ref, forcing_hbm, precond_hbm, off_hbm, diag_hbm, part_hbm, slot_hbm, perm_hbm,
    adjoint_ref, sent_ref, target_ref, place_ref,
    forcing_ref, precond_ref, kept_ref, diag_ref,
    part_ref, slot_ref, perm_ref, tails_ref, sems, off_sems,
):
    part_rows = perm_ref.shape[1]
    faces, elements = part_ref.shape
    whole = [
        pltpu.make_async_copy(source, target, sems.at[i])
        for i, (source, target) in enumerate(
            (
                (forcing_hbm, forcing_ref),
                (precond_hbm, precond_ref),
                (part_hbm, part_ref),
                (slot_hbm, slot_ref),
                (perm_hbm, perm_ref),
            )
        )
    ]
    diag_copy = pltpu.make_async_copy(diag_hbm, diag_ref, sems.at[5])
    queue = [
        pltpu.make_async_copy(off_hbm.at[e], kept_ref.at[e], off_sems.at[e])
        for e in range(elements)
    ] + [diag_copy]
    for copy in whole + queue[:ahead]:
        copy.start()
    adjoint_ref[...] = jnp.zeros(adjoint_ref.shape, F32)
    for copy in whole:
        copy.wait()
    block_products(forcing_ref, precond_ref, adjoint_ref)
    perm = perm_ref[...]
    rank = (perm * (65536 // elements + 1)) >> 16
    place_ref[...] = rank * PAD_ROWS + perm - rank * elements + 1
    target = face_targets(part_ref, slot_ref, my_part_ref[0], part_rows)
    target_ref[...] = target
    store_target(target, sent_ref, faces * elements)

    def arrived(e):
        if e + ahead < len(queue):
            queue[e + ahead].start()
        queue[e].wait()

    face_products(adjoint_ref, kept_ref, sent_ref, tails_ref, arrived)
    diag_copy.wait()


def rest_kernel(forcing_ref, adjoint_ref, diag_ref, rest_ref):
    elements, width = forcing_ref.shape
    rest_ref[...] = jnp.zeros(rest_ref.shape, F32)
    block_products(adjoint_ref, diag_ref, rest_ref)
    rest_ref[0:elements, 0:width] = forcing_ref[...] - rest_ref[0:elements, 0:width]


def pack_rows(buffers, table, rows_ref, out_ref):
    count = buffers[0].shape[0] - 2 * TAIL_STEP
    ranks = out_ref.shape[0]
    rows_ref[...] = jnp.zeros(rows_ref.shape, F32)
    tails = jnp.zeros((TAIL_STEP, WIDE), F32)
    for i, buffer in enumerate(buffers):
        rows_ref[i * count : (i + 1) * count, :] = buffer[0:count, :]
        tail = jnp.pad(buffer[count : count + TAIL_STEP, :], ((0, 0), (0, WIDE - LANES)))
        tails = tails + (pltpu.roll(tail, i * count, 1) if i else tail)
    high, low = split(rows_ref[...])
    main = jnp.dot(table, high, preferred_element_type=F32) + jnp.dot(
        table, low, preferred_element_type=F32
    )
    high, low = split(jnp.pad(tails, ((0, LANES - TAIL_STEP), (0, 0))))
    tail = contract(table, high) + contract(table, low)
    moved = pltpu.roll(tail, 0, 1, stride=TAIL_STEP, stride_axis=0)
    row = iota((PAD_ROWS, LANES), 0)
    for r in range(ranks):
        at = slice(r * PAD_ROWS, (r + 1) * PAD_ROWS)
        packed = jnp.sum(moved[at], axis=0, keepdims=True)
        out_ref[r] = jnp.where(row == PAD_ROWS - 4, packed, main[at])


def pack_kernel_first(
    own_ref, chip_ref, next_ref, target_ref, place_ref, out_ref, table_ref, rows_ref
):
    count = own_ref.shape[0] - 2 * TAIL_STEP
    part_rows = place_ref.shape[1]
    lane = iota((1, WIDE), 1)
    wanted = jnp.full((1, WIDE), -1, jnp.int32)
    for i, target in enumerate(
        (
            target_ref[...],
            chip_ref[count + TAIL_STEP : count + TAIL_STEP + 1, :].astype(jnp.int32),
            next_ref[count + TAIL_STEP : count + TAIL_STEP + 1, :].astype(jnp.int32),
        )
    ):
        slot = jnp.pad(target - i * part_rows, ((0, 0), (0, WIDE - LANES)))
        slot = pltpu.roll(slot, i * count, 1) if i else slot
        inside = jnp.logical_and(lane >= i * count, lane < (i + 1) * count)
        wanted = jnp.where(inside, slot, wanted)
    slots = (iota((part_rows, WIDE), 0) == wanted).astype(F32).astype(BF16)
    place = jnp.broadcast_to(place_ref[...].astype(F32), (TAIL_STEP, part_rows)).astype(BF16)
    position = jnp.dot(place, slots, preferred_element_type=F32)[0:1].astype(jnp.int32)
    table = (iota(table_ref.shape, 0) + 1 == position).astype(F32).astype(BF16)
    table_ref[...] = table
    pack_rows((own_ref, chip_ref, next_ref), table, rows_ref, out_ref)


def pack_kernel_next(own_ref, chip_ref, next_ref, table_ref, out_ref, rows_ref):
    pack_rows((own_ref, chip_ref, next_ref), table_ref[...], rows_ref, out_ref)


def gathered_rows(arrived_ref, width):
    total = arrived_ref[0]
    for r in range(1, arrived_ref.shape[0]):
        total = total + arrived_ref[r]
    packed = total[PAD_ROWS - 4 : PAD_ROWS - 3]
    tail = jnp.broadcast_to(packed, (PAD_ROWS, LANES))
    row = iota((PAD_ROWS, LANES), 0)
    for r in range(1, PAD_ROWS - 4):
        tail = jnp.where(row == r, pltpu.roll(packed, LANES - TAIL_STEP * r, 1), tail)
    tail = jnp.where(iota((PAD_ROWS, LANES), 1) < width - LANES, tail, 0.0)
    return jnp.concatenate([total, tail], axis=1)


def next_kernel(
    arrived_ref, rest_ref, before_ref, precond_ref, blocks_ref, target_ref,
    adjoint_ref, sent_ref, residual_ref, tails_ref,
):
    elements, faces, width = blocks_ref.shape[:3]
    residual_ref[...] = rest_ref[...] - gathered_rows(arrived_ref, width)
    adjoint_ref[...] = jnp.zeros(adjoint_ref.shape, F32)
    block_products(residual_ref, precond_ref, adjoint_ref)
    adjoint_ref[...] = before_ref[...] + adjoint_ref[...]
    store_target(target_ref[...], sent_ref, faces * elements)
    face_products(adjoint_ref, blocks_ref, sent_ref, tails_ref, lambda e: None)


def last_kernel(
    arrived_ref, rest_ref, before_ref, precond_ref, adjoint_ref, residual_ref, held_ref, sum_ref
):
    elements, width = residual_ref.shape
    held_ref[...] = rest_ref[...] - gathered_rows(arrived_ref, width)
    residual_ref[...] = held_ref[0:elements, 0:width]
    block_products(held_ref, precond_ref, sum_ref)
    adjoint_ref[...] = before_ref[0:elements, 0:width] + sum_ref[0:elements, 0:width]


def in_hbm(*arrays):
    return [pltpu.with_memory_space_constraint(a, pltpu.HBM) for a in arrays]


def cost(flops):
    return pl.CostEstimate(flops=flops, bytes_accessed=1 << 20, transcendentals=0)


def make_calls(elements, faces, width, ranks, ahead=6):
    part_rows = elements * ranks
    vector = pltpu.VMEM((PAD_ROWS, WIDE), F32)
    sent = pltpu.VMEM((faces * elements + 2 * TAIL_STEP, LANES), F32)
    tails = pltpu.VMEM((LANES, LANES), F32)
    hbm = pl.BlockSpec(memory_space=pltpu.HBM)
    smem = pl.BlockSpec(memory_space=pltpu.SMEM)
    out = jax.ShapeDtypeStruct((elements, width), F32)
    blocks = pltpu.VMEM((elements, width, width), BF16)
    perm = pltpu.VMEM((1, part_rows), jnp.int32)
    kept = (
        pltpu.VMEM((elements, width), F32),
        blocks,
        pltpu.VMEM((elements, faces, width, width), BF16),
        blocks,
    )
    indices = pltpu.VMEM((faces, elements), jnp.int32)
    packed = pltpu.VMEM((ranks, PAD_ROWS, LANES), F32)
    rows = pltpu.VMEM((WIDE, LANES), F32)
    table = pltpu.VMEM((ranks * PAD_ROWS, WIDE), BF16)
    first = pl.pallas_call(
        functools.partial(first_kernel, ahead),
        out_shape=(vector, sent, pltpu.VMEM((1, LANES), jnp.int32), perm, *kept),
        in_specs=[smem] + [hbm] * 7,
        scratch_shapes=[
            indices,
            indices,
            perm,
            tails,
            pltpu.SemaphoreType.DMA((6,)),
            pltpu.SemaphoreType.DMA((elements,)),
        ],
        compiler_params=PARAMS,
        name="first",
    )
    rest = pl.pallas_call(
        rest_kernel,
        out_shape=vector,
        compiler_params=PARAMS,
        cost_estimate=cost(10**9),
        name="rest",
    )
    pack_first = pl.pallas_call(
        pack_kernel_first,
        out_shape=(packed, table),
        scratch_shapes=[rows],
        compiler_params=PARAMS,
        name="pack_first",
    )
    pack_next = pl.pallas_call(
        pack_kernel_next,
        out_shape=packed,
        scratch_shapes=[rows],
        compiler_params=PARAMS,
        name="pack_next",
    )
    following = pl.pallas_call(
        next_kernel,
        out_shape=(vector, sent),
        scratch_shapes=[vector, tails],
        compiler_params=PARAMS,
        name="following",
    )
    last = pl.pallas_call(
        last_kernel,
        out_shape=(out, out),
        scratch_shapes=[vector] * 2,
        compiler_params=PARAMS,
        name="last",
    )
    return first, rest, pack_first, pack_next, following, last


def shards(forcing, diag_blocks, off_blocks, precond, face_part, face_slot, row_perm):
    elements, width = forcing.shape
    faces = face_part.shape[0]
    ranks = lax.axis_size("grp")
    parts = lax.axis_size("dom")
    first, rest_of, pack_first, pack_next, following, last = make_calls(
        elements, faces, width, ranks
    )
    my_part = lax.axis_index("dom").astype(jnp.int32).reshape(1)
    on_chip = [(p, p ^ 1) for p in range(parts)]
    across = [(p, ((p + 1) ^ 1) - 1) for p in range(1, parts - 1)]

    def exchange(sent, *rest_operands):
        from_beyond = lax.ppermute(sent, "dom", across)
        from_chip = lax.ppermute(sent, "dom", on_chip)
        return from_chip, from_beyond, rest_of(*rest_operands)

    adjoint, sent, target, place, forcing, precond, kept, diag_blocks = first(
        my_part,
        *in_hbm(forcing, precond, off_blocks, diag_blocks, face_part, face_slot, row_perm),
    )
    *received, rest = exchange(sent, forcing, adjoint, diag_blocks)
    outgoing, table = pack_first(sent, *received, target, place)
    arrived = lax.all_to_all(outgoing, "grp", 0, 0)

    adjoint, sent = following(arrived, rest, adjoint, precond, kept, target)
    *received, rest = exchange(sent, forcing, adjoint, diag_blocks)
    arrived = lax.all_to_all(pack_next(sent, *received, table), "grp", 0, 0)
    return last(arrived, rest, adjoint, precond)


def solution(mesh):
    return jax.shard_map(
        shards,
        mesh=mesh,
        in_specs=(
            P(("dom", "grp"), None),
            P(("dom", "grp"), None, None),
            P(("dom", "grp"), None, None, None),
            P(("dom", "grp"), None, None),
            P(None, ("dom", "grp")),
            P(None, ("dom", "grp")),
            P("dom", None),
        ),
        out_specs=(P(("dom", "grp"), None), P(("dom", "grp"), None)),
        check_vma=False,
    )
```

time: 59.8 us -> 63.6 us (1.064)
  blocking collectives: 19.1 us -> 0 us
  waiting for transfers between devices: 8.36 us -> 18.9 us
  starting transfers between devices: 22.9 us -> 30 us
  local copies, waits for them, and re-layouts: 0 us -> 4.66 us
    all_to_all x2 -> x0, blocking collectives: 19.1 us -> none  [shards(): lax.all_to_all(pack(own, from_chip, from_beyond, place), 'grp', 0, 0)]
    all_to_all x0 -> x2, waiting for transfers between devices: none -> 13.1 us  [the longest x1 6.57 us: shards(): arrived = lax.all_to_all(outgoing, 'grp', 0, 0)]
    all_to_all x0 -> x2, starting transfers between devices: none -> 7.02 us  [the longest x1 3.51 us: shards(): arrived = lax.all_to_all(outgoing, 'grp', 0, 0)]
    unnamed x0 -> x4, local copies, waits for them, and re-layouts: none -> 4.66 us
    ppermute x4, waiting for transfers between devices: 8.36 us -> 5.71 us  [the longest x2 5.7 us: exchange(): from_beyond = lax.ppermute(sent, 'dom', across)]
    pallas_call x5, Pallas kernels: 2.55 us -> 3.88 us  [the longest x1 1.26 us: shards(): outgoing, table = pack_first(sent, *received, target, place)]
    pallas_call x1, Pallas kernels: 4.9 us -> 4.17 us  [shards(): first(my_part, *in_hbm(forcing, precond, off_blocks, diag_blocks, face_pa...]
  transfers between devices with their start and end apart: 4 -> 6, of which waited for: 2 -> 4; matrix products, arithmetic and copies ran while one was open for 0% -> 0% of each run, Pallas kernels for 1% -> 1%
where the time goes in v4:
time: 63.6 us; the launch traced here: 63.2 us
  starting transfers between devices  30 us (47%)
  waiting for transfers between devices  18.9 us (30%)
  Pallas kernels  8.98 us (14%)
  local copies, waits for them, and re-layouts  4.66 us (7%)
  between operations  0.72 us (1%)
    ppermute x2, starting transfers between devices, exchange(): from_chip = lax.ppermute(sent, 'dom', on_chip)  17.9 us
    all_to_all x1, waiting for transfers between devices, shards(): arrived = lax.all_to_all(outgoing, 'grp', 0, 0)  6.57 us
    all_to_all x1, waiting for transfers between devices, shards(): arrived = lax.all_to_all(pack_next(sent, *received, table), 'grp', 0, 0)  6.57 us
    ppermute x2, waiting for transfers between devices, exchange(): from_beyond = lax.ppermute(sent, 'dom', across)  5.7 us
    ppermute x2, starting transfers between devices, exchange(): from_beyond = lax.ppermute(sent, 'dom', across)  4.99 us
    unnamed x4, local copies, waits for them, and re-layouts  4.66 us
    pallas_call x1, Pallas kernels, shards(): first(my_part, *in_hbm(forcing, precond, off_blocks, diag_blocks, face_pa...  4.17 us
    all_to_all x1, starting transfers between devices, shards(): arrived = lax.all_to_all(outgoing, 'grp', 0, 0)  3.51 us
  transfers between devices with their start and end apart: 6, of which 4 were waited for; matrix products, arithmetic and copies ran while one was open for 0% of the time, Pallas kernels for 1%

profile of v4, /device:TPU:1, one launch (start us, length us, event | category | flops | bytes accessed | tf_op | source)
XLA Modules:
  0.0 63.2 jit_solution(1812978832289808921)
XLA Ops:
  0.6 4.2 %first.1 = (f32[16,256]{1,0:T(8,128)S(1)}, f32[88,128]{1,0:T(8,128)S(1)}, s32[1,128]{1,0:T(1,128)S(1)}, s32[1,192]{1,0:T(1,128)S(1)}, f32[12,135]{1,0:T(8,128)S(...) custom-call(s32[1]{0:T(128)} %bitcast.my_part_ref, ...), custom_call_target="tpu_custom_call" | custom-call | tf_op jit(solution)/shard_map/first/pallas_call | solution.py:317
  4.8 0.0 copy-start
  4.8 2.2 %copy-done = bf16[12,6,135,135]{3,2,1,0:T(8,128)(2,1)} copy-done((bf16[12,6,135,135]{3,2,1,0:T(8,128)(2,1)}, bf16[12,6,135,135]{3,2,1,0:T(8,128)(2,1)S(1)}, u32[]{:S(2)}) %copy-start) | copy-done | bytes 2624424
  7.1 16.0 %collective-permute-start = (f32[88,128]{1,0:T(8,128)S(1)}, f32[88,128]{1,0:T(8,128)S(1)}, u32[]{:S(2)}, u32[]{:S(2)}) collective-permute-start(f32[88,128]{1,0:T(8,128)S(1)} %get-tuple-element.14.own_ref), channel_id=1, source_target_pairs={{0,16},{16,0},{32,48},{48,32},{64,80},{80,64},{96,112},{112,96},{1... | collective-permute-start | bytes 135176 | tf_op jit(solution)/shard_map/ppermute | solution.py:314
  23.1 1.9 %collective-permute-start.1 = (f32[88,128]{1,0:T(8,128)S(1)}, f32[88,128]{1,0:T(8,128)S(1)}, u32[]{:S(2)}, u32[]{:S(2)}) collective-permute-start(f32[88,128]{1,0:T(8,128)S(1)} %get-tuple-element.14.own_ref), channel_id=1, source_target_pairs={{16,32},{32,16},{48,64},{64,48},{80,96},{96,80},{112,128},{128,112... | collective-permute-start | bytes 135176 | tf_op jit(solution)/shard_map/ppermute | solution.py:313
  25.0 0.0 collective-permute-done.chip_ref
  25.0 3.4 %collective-permute-done.1.next_ref = f32[88,128]{1,0:T(8,128)S(1)} collective-permute-done((f32[88,128]{1,0:T(8,128)S(1)}, f32[88,128]{1,0:T(8,128)S(1)}, u32[]{:S(2)}, u32[]{:S(2)}) %collective-permute-start.1) | collective-permute-done | bytes 45088 | tf_op jit(solution)/shard_map/ppermute | solution.py:313
  28.4 1.3 %pack_first.1 = (f32[16,16,128]{2,1,0:T(8,128)}, bf16[256,256]{1,0:T(8,128)(2,1)S(1)}) custom-call(f32[88,128]{1,0:T(8,128)S(1)} %get-tuple-element.14.own_ref, f32[88,128]{1,0:T(8,128)S(1)} %collective-permute-done.chip_ref, f32[88,128]{1,0:T(8,128)S(1)} %collective-permute-done.1.next_ref, s32[1,128]{1,0:T(1,128)S(1)} %get-tuple-element.15.target_ref, ...), custom_call_target="tpu_custom_call" | custom-call | tf_op jit(solution)/shard_map/pack_first/pallas_call | solution.py:322
  29.7 3.5 %all-to-all-start = ((f32[16,16,128]{2,1,0:T(8,128)}), f32[16,16,128]{2,1,0:T(8,128)S(1)}, u32[]{:S(2)}, u32[]{:S(2)}) async-start(f32[16,16,128]{2,1,0:T(8,128)} %get-tuple-element.17), calls=%async_computation | async-start | bytes 262144 | tf_op jit(solution)/shard_map/all_to_all | solution.py:323
  33.2 0.2 rest.2.rest_ref
  33.5 6.6 %all-to-all-done.arrived_ref = f32[16,16,128]{2,1,0:T(8,128)S(1)} async-done(((f32[16,16,128]{2,1,0:T(8,128)}), f32[16,16,128]{2,1,0:T(8,128)S(1)}, u32[]{:S(2)}, u32[]{:S(2)}) %all-to-all-start) | async-done | bytes 131104 | tf_op jit(solution)/shard_map/all_to_all | solution.py:323
  40.0 0.0 copy-start.1
  40.0 2.4 %copy-done.1 = bf16[12,6,135,135]{3,2,1,0:T(8,128)(2,1)S(1)} copy-done((bf16[12,6,135,135]{3,2,1,0:T(8,128)(2,1)S(1)}, bf16[12,6,135,135]{3,2,1,0:T(8,128)(2,1)}, u32[]{:S(2)}) %copy-start.1) | copy-done | bytes 2624424
  42.5 1.1 %following.1 = (f32[16,256]{1,0:T(8,128)S(1)}, f32[88,128]{1,0:T(8,128)S(1)}) custom-call(f32[16,16,128]{2,1,0:T(8,128)S(1)} %all-to-all-done.arrived_ref, f32[16,256]{1,0:T(8,128)S(1)} %rest.2.rest_ref, f32[16,256]{1,0:T(8,128)S(1)} %get-tuple-element.19.adjoint_ref.before_ref, bf16[12,135,135]{2,1,0:T(8,128)(2,1)S(1)} %get-tuple-element.21.precond_ref, ...), custom_call_target="tpu_custom_call" | custom-call | tf_op jit(solution)/shard_map/following/pallas_call | solution.py:325
  43.6 1.9 %collective-permute-start.2 = (f32[88,128]{1,0:T(8,128)S(1)}, f32[88,128]{1,0:T(8,128)S(1)}, u32[]{:S(2)}, u32[]{:S(2)}) collective-permute-start(f32[88,128]{1,0:T(8,128)S(1)} %get-tuple-element.23.own_ref), channel_id=1, source_target_pairs={{0,16},{16,0},{32,48},{48,32},{64,80},{80,64},{96,112},{112,96},{1... | collective-permute-start | bytes 135176 | tf_op jit(solution)/shard_map/ppermute | solution.py:314
  45.5 3.1 %collective-permute-start.3 = (f32[88,128]{1,0:T(8,128)S(1)}, f32[88,128]{1,0:T(8,128)S(1)}, u32[]{:S(2)}, u32[]{:S(2)}) collective-permute-start(f32[88,128]{1,0:T(8,128)S(1)} %get-tuple-element.23.own_ref), channel_id=1, source_target_pairs={{16,32},{32,16},{48,64},{64,48},{80,96},{96,80},{112,128},{128,112... | collective-permute-start | bytes 135176 | tf_op jit(solution)/shard_map/ppermute | solution.py:313
  48.6 0.0 collective-permute-done.2.chip_ref
  48.6 2.3 %collective-permute-done.3.next_ref = f32[88,128]{1,0:T(8,128)S(1)} collective-permute-done((f32[88,128]{1,0:T(8,128)S(1)}, f32[88,128]{1,0:T(8,128)S(1)}, u32[]{:S(2)}, u32[]{:S(2)}) %collective-permute-start.3) | collective-permute-done | bytes 45088 | tf_op jit(solution)/shard_map/ppermute | solution.py:313
  50.9 1.1 %pack_next.1 = f32[16,16,128]{2,1,0:T(8,128)} custom-call(f32[88,128]{1,0:T(8,128)S(1)} %get-tuple-element.23.own_ref, f32[88,128]{1,0:T(8,128)S(1)} %collective-permute-done.2.chip_ref, f32[88,128]{1,0:T(8,128)S(1)} %collective-permute-done.3.next_ref, bf16[256,256]{1,0:T(8,128)(2,1)S(1)} %get-tuple-element.24.table_ref), custom_call_target="tpu_custom_call" | custom-call | tf_op jit(solution)/shard_map/pack_next/pallas_call | solution.py:327
  51.9 3.5 %all-to-all-start.1 = ((f32[16,16,128]{2,1,0:T(8,128)}), f32[16,16,128]{2,1,0:T(8,128)S(1)}, u32[]{:S(2)}, u32[]{:S(2)}) async-start(f32[16,16,128]{2,1,0:T(8,128)} %pack_next.1), calls=%async_computation.1 | async-start | bytes 262144 | tf_op jit(solution)/shard_map/all_to_all | solution.py:327
  55.4 0.2 rest.3.rest_ref
  55.7 6.6 %all-to-all-done.1.arrived_ref = f32[16,16,128]{2,1,0:T(8,128)S(1)} async-done(((f32[16,16,128]{2,1,0:T(8,128)}), f32[16,16,128]{2,1,0:T(8,128)S(1)}, u32[]{:S(2)}, u32[]{:S(2)}) %all-to-all-start.1) | async-done | bytes 131104 | tf_op jit(solution)/shard_map/all_to_all | solution.py:327
  62.2 0.9 %last.1 = (f32[12,135]{1,0:T(8,128)}, f32[12,135]{1,0:T(8,128)}) custom-call(f32[16,16,128]{2,1,0:T(8,128)S(1)} %all-to-all-done.1.arrived_ref, f32[16,256]{1,0:T(8,128)S(1)} %rest.3.rest_ref, f32[16,256]{1,0:T(8,128)S(1)} %get-tuple-element.25.adjoint_ref.before_ref, bf16[12,135,135]{2,1,0:T(8,128)(2,1)S(1)} %get-tuple-element.21.precond_ref), custom_call_target="tpu_custom_call" | custom-call | tf_op jit(solution)/shard_map/last/pallas_call | solution.py:328
Async XLA Ops:
  4.8 2.2 %copy-start = (bf16[12,6,135,135]{3,2,1,0:T(8,128)(2,1)}, bf16[12,6,135,135]{3,2,1,0:T(8,128)(2,1)S(1)}, u32[]{:S(2)}) copy-start(bf16[12,6,135,135]{3,2,1,0:T(8,128)(2,1)S(1)} %get-tuple-element.22.blocks_ref) | copy-start | bytes 7873204
  7.1 17.9 %collective-permute-start = (f32[88,128]{1,0:T(8,128)S(1)}, f32[88,128]{1,0:T(8,128)S(1)}, u32[]{:S(2)}, u32[]{:S(2)}) collective-permute-start(f32[88,128]{1,0:T(8,128)S(1)} %get-tuple-element.14.own_ref), channel_id=1, source_target_pairs={{0,16},{16,0},{32,48},{48,32},{64,80},{80,64},{96,112},{112,96},{1... | collective-permute-start | bytes 135176 | tf_op jit(solution)/shard_map/ppermute | solution.py:314
  23.1 5.4 %collective-permute-start.1 = (f32[88,128]{1,0:T(8,128)S(1)}, f32[88,128]{1,0:T(8,128)S(1)}, u32[]{:S(2)}, u32[]{:S(2)}) collective-permute-start(f32[88,128]{1,0:T(8,128)S(1)} %get-tuple-element.14.own_ref), channel_id=1, source_target_pairs={{16,32},{32,16},{48,64},{64,48},{80,96},{96,80},{112,128},{128,112... | collective-permute-start | bytes 135176 | tf_op jit(solution)/shard_map/ppermute | solution.py:313
  29.7 10.3 %all-to-all-start = ((f32[16,16,128]{2,1,0:T(8,128)}), f32[16,16,128]{2,1,0:T(8,128)S(1)}, u32[]{:S(2)}, u32[]{:S(2)}) async-start(f32[16,16,128]{2,1,0:T(8,128)} %get-tuple-element.17), calls=%async_computation | async-start | bytes 262144 | tf_op jit(solution)/shard_map/all_to_all | solution.py:323
  40.0 2.4 %copy-start.1 = (bf16[12,6,135,135]{3,2,1,0:T(8,128)(2,1)S(1)}, bf16[12,6,135,135]{3,2,1,0:T(8,128)(2,1)}, u32[]{:S(2)}) copy-start(bf16[12,6,135,135]{3,2,1,0:T(8,128)(2,1)} %copy-done) | copy-start | bytes 7873204
  43.6 5.0 %collective-permute-start.2 = (f32[88,128]{1,0:T(8,128)S(1)}, f32[88,128]{1,0:T(8,128)S(1)}, u32[]{:S(2)}, u32[]{:S(2)}) collective-permute-start(f32[88,128]{1,0:T(8,128)S(1)} %get-tuple-element.23.own_ref), channel_id=1, source_target_pairs={{0,16},{16,0},{32,48},{48,32},{64,80},{80,64},{96,112},{112,96},{1... | collective-permute-start | bytes 135176 | tf_op jit(solution)/shard_map/ppermute | solution.py:314
  45.5 5.4 %collective-permute-start.3 = (f32[88,128]{1,0:T(8,128)S(1)}, f32[88,128]{1,0:T(8,128)S(1)}, u32[]{:S(2)}, u32[]{:S(2)}) collective-permute-start(f32[88,128]{1,0:T(8,128)S(1)} %get-tuple-element.23.own_ref), channel_id=1, source_target_pairs={{16,32},{32,16},{48,64},{64,48},{80,96},{96,80},{112,128},{128,112... | collective-permute-start | bytes 135176 | tf_op jit(solution)/shard_map/ppermute | solution.py:313
  51.9 10.3 %all-to-all-start.1 = ((f32[16,16,128]{2,1,0:T(8,128)}), f32[16,16,128]{2,1,0:T(8,128)S(1)}, u32[]{:S(2)}, u32[]{:S(2)}) async-start(f32[16,16,128]{2,1,0:T(8,128)} %pack_next.1), calls=%async_computation.1 | async-start | bytes 262144 | tf_op jit(solution)/shard_map/all_to_all | solution.py:327

commit v5 on v4

--- a/solution.py
+++ b/solution.py
@@ -54,6 +54,7 @@
 def face_targets(part_ref, slot_ref, my_part, part_rows):
     faces, elements = part_ref.shape
     part, slot = part_ref[...], slot_ref[...]
+    my_part = my_part[:, 0:elements]
     offset = part - my_part
     towards_chip = 1 - 2 * (my_part & 1)
     section = jnp.where(offset == 0, 0, jnp.where(offset == towards_chip, 1, 2))
@@ -94,27 +95,34 @@
         )
     ]
     diag_copy = pltpu.make_async_copy(diag_hbm, diag_ref, sems.at[5])
+    chunk = elements // off_sems.shape[0]
     queue = [
-        pltpu.make_async_copy(off_hbm.at[e], kept_ref.at[e], off_sems.at[e])
-        for e in range(elements)
+        pltpu.make_async_copy(
+            off_hbm.at[pl.ds(e, chunk)], kept_ref.at[pl.ds(e, chunk)], off_sems.at[e // chunk]
+        )
+        for e in range(0, elements, chunk)
     ] + [diag_copy]
-    for copy in whole + queue[:ahead]:
+    early, ahead, _ = ahead
+    for copy in whole + queue[:early]:
         copy.start()
     adjoint_ref[...] = jnp.zeros(adjoint_ref.shape, F32)
     for copy in whole:
         copy.wait()
+    for copy in queue[early:ahead]:
+        copy.start()
     block_products(forcing_ref, precond_ref, adjoint_ref)
     perm = perm_ref[...]
     rank = (perm * (65536 // elements + 1)) >> 16
     place_ref[...] = rank * PAD_ROWS + perm - rank * elements + 1
-    target = face_targets(part_ref, slot_ref, my_part_ref[0], part_rows)
+    target = face_targets(part_ref, slot_ref, my_part_ref[...], part_rows)
     target_ref[...] = target
     store_target(target, sent_ref, faces * elements)
 
     def arrived(e):
-        if e + ahead < len(queue):
-            queue[e + ahead].start()
-        queue[e].wait()
+        if e % chunk == 0:
+            if e // chunk + ahead < len(queue):
+                queue[e // chunk + ahead].start()
+            queue[e // chunk].wait()
 
     face_products(adjoint_ref, kept_ref, sent_ref, tails_ref, arrived)
     diag_copy.wait()
@@ -130,18 +138,20 @@
 def pack_rows(buffers, table, rows_ref, out_ref):
     count = buffers[0].shape[0] - 2 * TAIL_STEP
     ranks = out_ref.shape[0]
-    rows_ref[...] = jnp.zeros(rows_ref.shape, F32)
+    used = len(buffers) * count
+    rows_ref[used:, :] = jnp.zeros((WIDE - used, LANES), F32)
     tails = jnp.zeros((TAIL_STEP, WIDE), F32)
     for i, buffer in enumerate(buffers):
         rows_ref[i * count : (i + 1) * count, :] = buffer[0:count, :]
         tail = jnp.pad(buffer[count : count + TAIL_STEP, :], ((0, 0), (0, WIDE - LANES)))
         tails = tails + (pltpu.roll(tail, i * count, 1) if i else tail)
-    high, low = split(rows_ref[...])
-    main = jnp.dot(table, high, preferred_element_type=F32) + jnp.dot(
-        table, low, preferred_element_type=F32
-    )
+    both = jnp.dot(
+        table, jnp.concatenate(split(rows_ref[...]), axis=1), preferred_element_type=F32
+    )
+    main = both[:, 0:LANES] + both[:, LANES:WIDE]
     high, low = split(jnp.pad(tails, ((0, LANES - TAIL_STEP), (0, 0))))
-    tail = contract(table, high) + contract(table, low)
+    both = contract(table, jnp.concatenate([high, low], axis=0))
+    tail = both[:, 0:LANES] + both[:, LANES:WIDE]
     moved = pltpu.roll(tail, 0, 1, stride=TAIL_STEP, stride_axis=0)
     row = iota((PAD_ROWS, LANES), 0)
     for r in range(ranks):
@@ -224,13 +234,13 @@
     return pl.CostEstimate(flops=flops, bytes_accessed=1 << 20, transcendentals=0)
 
 
-def make_calls(elements, faces, width, ranks, ahead=6):
+def make_calls(elements, faces, width, ranks, ahead=(4, 5, 3)):
     part_rows = elements * ranks
     vector = pltpu.VMEM((PAD_ROWS, WIDE), F32)
     sent = pltpu.VMEM((faces * elements + 2 * TAIL_STEP, LANES), F32)
     tails = pltpu.VMEM((LANES, LANES), F32)
     hbm = pl.BlockSpec(memory_space=pltpu.HBM)
-    smem = pl.BlockSpec(memory_space=pltpu.SMEM)
+    vmem = pl.BlockSpec(memory_space=pltpu.VMEM)
     out = jax.ShapeDtypeStruct((elements, width), F32)
     blocks = pltpu.VMEM((elements, width, width), BF16)
     perm = pltpu.VMEM((1, part_rows), jnp.int32)
@@ -247,14 +257,14 @@
     first = pl.pallas_call(
         functools.partial(first_kernel, ahead),
         out_shape=(vector, sent, pltpu.VMEM((1, LANES), jnp.int32), perm, *kept),
-        in_specs=[smem] + [hbm] * 7,
+        in_specs=[vmem] + [hbm] * 7,
         scratch_shapes=[
             indices,
             indices,
             perm,
             tails,
             pltpu.SemaphoreType.DMA((6,)),
-            pltpu.SemaphoreType.DMA((elements,)),
+            pltpu.SemaphoreType.DMA((elements // ahead[2],)),
         ],
         compiler_params=PARAMS,
         name="first",
@@ -305,7 +315,8 @@
     first, rest_of, pack_first, pack_next, following, last = make_calls(
         elements, faces, width, ranks
     )
-    my_part = lax.axis_index("dom").astype(jnp.int32).reshape(1)
+    my_part = jnp.full((1, LANES), lax.axis_index("dom"), jnp.int32)
+    my_part = pltpu.with_memory_space_constraint(my_part, pltpu.VMEM)
     on_chip = [(p, p ^ 1) for p in range(parts)]
     across = [(p, ((p + 1) ^ 1) - 1) for p in range(1, parts - 1)]
 

time: 63.6 us -> 63.1 us (level)
  no operation moved by 1% of the time
where the time goes in v5:
time: 63.1 us; the launch traced here: 62.6 us
  starting transfers between devices  30 us (48%)
  waiting for transfers between devices  18.9 us (30%)
  Pallas kernels  8.39 us (13%)
  local copies, waits for them, and re-layouts  4.66 us (7%)
  between operations  0.73 us (1%)
    ppermute x2, starting transfers between devices, exchange(): from_chip = lax.ppermute(sent, 'dom', on_chip)  17.9 us
    all_to_all x1, waiting for transfers between devices, shards(): arrived = lax.all_to_all(outgoing, 'grp', 0, 0)  6.57 us
    all_to_all x1, waiting for transfers between devices, shards(): arrived = lax.all_to_all(pack_next(sent, *received, table), 'grp', 0, 0)  6.57 us
    ppermute x2, waiting for transfers between devices, exchange(): from_beyond = lax.ppermute(sent, 'dom', across)  5.7 us
    ppermute x2, starting transfers between devices, exchange(): from_beyond = lax.ppermute(sent, 'dom', across)  4.99 us
    unnamed x4, local copies, waits for them, and re-layouts  4.66 us
    pallas_call x1, Pallas kernels, shards(): first(my_part, *in_hbm(forcing, precond, off_blocks, diag_blocks, face_pa...  3.66 us
    all_to_all x1, starting transfers between devices, shards(): arrived = lax.all_to_all(outgoing, 'grp', 0, 0)  3.51 us
  transfers between devices with their start and end apart: 6, of which 4 were waited for; matrix products, arithmetic and copies ran while one was open for 0% of the time, Pallas kernels for 1%

profile of v5, /device:TPU:1, one launch (start us, length us, event | category | flops | bytes accessed | tf_op | source)
XLA Modules:
  0.0 62.6 jit_solution(3319023427128718125)
XLA Ops:
  0.6 3.7 %first.1 = (f32[16,256]{1,0:T(8,128)S(1)}, f32[88,128]{1,0:T(8,128)S(1)}, s32[1,128]{1,0:T(1,128)S(1)}, s32[1,192]{1,0:T(1,128)S(1)}, f32[12,135]{1,0:T(8,128)S(...) custom-call(s32[1,128]{1,0:T(1,128)S(1)} %broadcast_in_dim.3.my_part, ...), custom_call_target="tpu_custom_call" | custom-call | tf_op jit(solution)/shard_map/first/pallas_call | solution.py:328
  4.3 0.0 copy-start
  4.3 2.2 %copy-done = bf16[12,6,135,135]{3,2,1,0:T(8,128)(2,1)} copy-done((bf16[12,6,135,135]{3,2,1,0:T(8,128)(2,1)}, bf16[12,6,135,135]{3,2,1,0:T(8,128)(2,1)S(1)}, u32[]{:S(2)}) %copy-start) | copy-done | bytes 2624424
  6.6 16.0 %collective-permute-start = (f32[88,128]{1,0:T(8,128)S(1)}, f32[88,128]{1,0:T(8,128)S(1)}, u32[]{:S(2)}, u32[]{:S(2)}) collective-permute-start(f32[88,128]{1,0:T(8,128)S(1)} %get-tuple-element.14.own_ref), channel_id=1, source_target_pairs={{0,16},{16,0},{32,48},{48,32},{64,80},{80,64},{96,112},{112,96},{1... | collective-permute-start | bytes 135176 | tf_op jit(solution)/shard_map/ppermute | solution.py:325
  22.6 1.9 %collective-permute-start.1 = (f32[88,128]{1,0:T(8,128)S(1)}, f32[88,128]{1,0:T(8,128)S(1)}, u32[]{:S(2)}, u32[]{:S(2)}) collective-permute-start(f32[88,128]{1,0:T(8,128)S(1)} %get-tuple-element.14.own_ref), channel_id=1, source_target_pairs={{16,32},{32,16},{48,64},{64,48},{80,96},{96,80},{112,128},{128,112... | collective-permute-start | bytes 135176 | tf_op jit(solution)/shard_map/ppermute | solution.py:324
  24.5 0.0 collective-permute-done.chip_ref
  24.5 3.4 %collective-permute-done.1.next_ref = f32[88,128]{1,0:T(8,128)S(1)} collective-permute-done((f32[88,128]{1,0:T(8,128)S(1)}, f32[88,128]{1,0:T(8,128)S(1)}, u32[]{:S(2)}, u32[]{:S(2)}) %collective-permute-start.1) | collective-permute-done | bytes 45088 | tf_op jit(solution)/shard_map/ppermute | solution.py:324
  27.9 1.2 %pack_first.1 = (f32[16,16,128]{2,1,0:T(8,128)}, bf16[256,256]{1,0:T(8,128)(2,1)S(1)}) custom-call(f32[88,128]{1,0:T(8,128)S(1)} %get-tuple-element.14.own_ref, f32[88,128]{1,0:T(8,128)S(1)} %collective-permute-done.chip_ref, f32[88,128]{1,0:T(8,128)S(1)} %collective-permute-done.1.next_ref, s32[1,128]{1,0:T(1,128)S(1)} %get-tuple-element.15.target_ref, ...), custom_call_target="tpu_custom_call" | custom-call | tf_op jit(solution)/shard_map/pack_first/pallas_call | solution.py:333
  29.1 3.5 %all-to-all-start = ((f32[16,16,128]{2,1,0:T(8,128)}), f32[16,16,128]{2,1,0:T(8,128)S(1)}, u32[]{:S(2)}, u32[]{:S(2)}) async-start(f32[16,16,128]{2,1,0:T(8,128)} %get-tuple-element.17), calls=%async_computation | async-start | bytes 262144 | tf_op jit(solution)/shard_map/all_to_all | solution.py:334
  32.6 0.2 rest.2.rest_ref
  32.9 6.6 %all-to-all-done.arrived_ref = f32[16,16,128]{2,1,0:T(8,128)S(1)} async-done(((f32[16,16,128]{2,1,0:T(8,128)}), f32[16,16,128]{2,1,0:T(8,128)S(1)}, u32[]{:S(2)}, u32[]{:S(2)}) %all-to-all-start) | async-done | bytes 131104 | tf_op jit(solution)/shard_map/all_to_all | solution.py:334
  39.5 0.0 copy-start.1
  39.5 2.4 %copy-done.1 = bf16[12,6,135,135]{3,2,1,0:T(8,128)(2,1)S(1)} copy-done((bf16[12,6,135,135]{3,2,1,0:T(8,128)(2,1)S(1)}, bf16[12,6,135,135]{3,2,1,0:T(8,128)(2,1)}, u32[]{:S(2)}) %copy-start.1) | copy-done | bytes 2624424
  41.9 1.1 %following.1 = (f32[16,256]{1,0:T(8,128)S(1)}, f32[88,128]{1,0:T(8,128)S(1)}) custom-call(f32[16,16,128]{2,1,0:T(8,128)S(1)} %all-to-all-done.arrived_ref, f32[16,256]{1,0:T(8,128)S(1)} %rest.2.rest_ref, f32[16,256]{1,0:T(8,128)S(1)} %get-tuple-element.19.adjoint_ref.before_ref, bf16[12,135,135]{2,1,0:T(8,128)(2,1)S(1)} %get-tuple-element.21.precond_ref, ...), custom_call_target="tpu_custom_call" | custom-call | tf_op jit(solution)/shard_map/following/pallas_call | solution.py:336
  43.0 1.9 %collective-permute-start.2 = (f32[88,128]{1,0:T(8,128)S(1)}, f32[88,128]{1,0:T(8,128)S(1)}, u32[]{:S(2)}, u32[]{:S(2)}) collective-permute-start(f32[88,128]{1,0:T(8,128)S(1)} %get-tuple-element.23.own_ref), channel_id=1, source_target_pairs={{0,16},{16,0},{32,48},{48,32},{64,80},{80,64},{96,112},{112,96},{1... | collective-permute-start | bytes 135176 | tf_op jit(solution)/shard_map/ppermute | solution.py:325
  44.9 3.1 %collective-permute-start.3 = (f32[88,128]{1,0:T(8,128)S(1)}, f32[88,128]{1,0:T(8,128)S(1)}, u32[]{:S(2)}, u32[]{:S(2)}) collective-permute-start(f32[88,128]{1,0:T(8,128)S(1)} %get-tuple-element.23.own_ref), channel_id=1, source_target_pairs={{16,32},{32,16},{48,64},{64,48},{80,96},{96,80},{112,128},{128,112... | collective-permute-start | bytes 135176 | tf_op jit(solution)/shard_map/ppermute | solution.py:324
  48.0 0.0 collective-permute-done.2.chip_ref
  48.0 2.3 %collective-permute-done.3.next_ref = f32[88,128]{1,0:T(8,128)S(1)} collective-permute-done((f32[88,128]{1,0:T(8,128)S(1)}, f32[88,128]{1,0:T(8,128)S(1)}, u32[]{:S(2)}, u32[]{:S(2)}) %collective-permute-start.3) | collective-permute-done | bytes 45088 | tf_op jit(solution)/shard_map/ppermute | solution.py:324
  50.3 1.0 %pack_next.1 = f32[16,16,128]{2,1,0:T(8,128)} custom-call(f32[88,128]{1,0:T(8,128)S(1)} %get-tuple-element.23.own_ref, f32[88,128]{1,0:T(8,128)S(1)} %collective-permute-done.2.chip_ref, f32[88,128]{1,0:T(8,128)S(1)} %collective-permute-done.3.next_ref, bf16[256,256]{1,0:T(8,128)(2,1)S(1)} %get-tuple-element.24.table_ref), custom_call_target="tpu_custom_call" | custom-call | tf_op jit(solution)/shard_map/pack_next/pallas_call | solution.py:338
  51.3 3.5 %all-to-all-start.1 = ((f32[16,16,128]{2,1,0:T(8,128)}), f32[16,16,128]{2,1,0:T(8,128)S(1)}, u32[]{:S(2)}, u32[]{:S(2)}) async-start(f32[16,16,128]{2,1,0:T(8,128)} %pack_next.1), calls=%async_computation.1 | async-start | bytes 262144 | tf_op jit(solution)/shard_map/all_to_all | solution.py:338
  54.9 0.2 rest.3.rest_ref
  55.1 6.6 %all-to-all-done.1.arrived_ref = f32[16,16,128]{2,1,0:T(8,128)S(1)} async-done(((f32[16,16,128]{2,1,0:T(8,128)}), f32[16,16,128]{2,1,0:T(8,128)S(1)}, u32[]{:S(2)}, u32[]{:S(2)}) %all-to-all-start.1) | async-done | bytes 131104 | tf_op jit(solution)/shard_map/all_to_all | solution.py:338
  61.7 0.9 %last.1 = (f32[12,135]{1,0:T(8,128)}, f32[12,135]{1,0:T(8,128)}) custom-call(f32[16,16,128]{2,1,0:T(8,128)S(1)} %all-to-all-done.1.arrived_ref, f32[16,256]{1,0:T(8,128)S(1)} %rest.3.rest_ref, f32[16,256]{1,0:T(8,128)S(1)} %get-tuple-element.25.adjoint_ref.before_ref, bf16[12,135,135]{2,1,0:T(8,128)(2,1)S(1)} %get-tuple-element.21.precond_ref), custom_call_target="tpu_custom_call" | custom-call | tf_op jit(solution)/shard_map/last/pallas_call | solution.py:339
  (1 shorter events, 0.0 us)
Async XLA Ops:
  4.3 2.2 %copy-start = (bf16[12,6,135,135]{3,2,1,0:T(8,128)(2,1)}, bf16[12,6,135,135]{3,2,1,0:T(8,128)(2,1)S(1)}, u32[]{:S(2)}) copy-start(bf16[12,6,135,135]{3,2,1,0:T(8,128)(2,1)S(1)} %get-tuple-element.22.blocks_ref) | copy-start | bytes 7873204
  6.6 17.9 %collective-permute-start = (f32[88,128]{1,0:T(8,128)S(1)}, f32[88,128]{1,0:T(8,128)S(1)}, u32[]{:S(2)}, u32[]{:S(2)}) collective-permute-start(f32[88,128]{1,0:T(8,128)S(1)} %get-tuple-element.14.own_ref), channel_id=1, source_target_pairs={{0,16},{16,0},{32,48},{48,32},{64,80},{80,64},{96,112},{112,96},{1... | collective-permute-start | bytes 135176 | tf_op jit(solution)/shard_map/ppermute | solution.py:325
  22.6 5.4 %collective-permute-start.1 = (f32[88,128]{1,0:T(8,128)S(1)}, f32[88,128]{1,0:T(8,128)S(1)}, u32[]{:S(2)}, u32[]{:S(2)}) collective-permute-start(f32[88,128]{1,0:T(8,128)S(1)} %get-tuple-element.14.own_ref), channel_id=1, source_target_pairs={{16,32},{32,16},{48,64},{64,48},{80,96},{96,80},{112,128},{128,112... | collective-permute-start | bytes 135176 | tf_op jit(solution)/shard_map/ppermute | solution.py:324
  29.1 10.3 %all-to-all-start = ((f32[16,16,128]{2,1,0:T(8,128)}), f32[16,16,128]{2,1,0:T(8,128)S(1)}, u32[]{:S(2)}, u32[]{:S(2)}) async-start(f32[16,16,128]{2,1,0:T(8,128)} %get-tuple-element.17), calls=%async_computation | async-start | bytes 262144 | tf_op jit(solution)/shard_map/all_to_all | solution.py:334
  39.5 2.4 %copy-start.1 = (bf16[12,6,135,135]{3,2,1,0:T(8,128)(2,1)S(1)}, bf16[12,6,135,135]{3,2,1,0:T(8,128)(2,1)}, u32[]{:S(2)}) copy-start(bf16[12,6,135,135]{3,2,1,0:T(8,128)(2,1)} %copy-done) | copy-start | bytes 7873204
  43.0 5.0 %collective-permute-start.2 = (f32[88,128]{1,0:T(8,128)S(1)}, f32[88,128]{1,0:T(8,128)S(1)}, u32[]{:S(2)}, u32[]{:S(2)}) collective-permute-start(f32[88,128]{1,0:T(8,128)S(1)} %get-tuple-element.23.own_ref), channel_id=1, source_target_pairs={{0,16},{16,0},{32,48},{48,32},{64,80},{80,64},{96,112},{112,96},{1... | collective-permute-start | bytes 135176 | tf_op jit(solution)/shard_map/ppermute | solution.py:325
  44.9 5.4 %collective-permute-start.3 = (f32[88,128]{1,0:T(8,128)S(1)}, f32[88,128]{1,0:T(8,128)S(1)}, u32[]{:S(2)}, u32[]{:S(2)}) collective-permute-start(f32[88,128]{1,0:T(8,128)S(1)} %get-tuple-element.23.own_ref), channel_id=1, source_target_pairs={{16,32},{32,16},{48,64},{64,48},{80,96},{96,80},{112,128},{128,112... | collective-permute-start | bytes 135176 | tf_op jit(solution)/shard_map/ppermute | solution.py:324
  51.3 10.3 %all-to-all-start.1 = ((f32[16,16,128]{2,1,0:T(8,128)}), f32[16,16,128]{2,1,0:T(8,128)S(1)}, u32[]{:S(2)}, u32[]{:S(2)}) async-start(f32[16,16,128]{2,1,0:T(8,128)} %pack_next.1), calls=%async_computation.1 | async-start | bytes 262144 | tf_op jit(solution)/shard_map/all_to_all | solution.py:338
